TPU v7x, 512 devices: a whole 4x4x16 slice. The times are simulated.
512 devices in a mesh: section: 2 (over core), dp: 64 (over z, y), mp: 4 (over x).
Axes of the slice: x: 4, y: 4, z: 16, core: 2. Of those that a mesh axis runs over, the one named last changes fastest.
Arguments:
- qkv: bfloat16 [8192, 3072], P('dp', ('section', 'mp')), may hold values from -6 to 6
- kv_cache: bfloat16 [4096, 8, 2048], P('dp', None, ('section', 'mp')), may hold values from -6 to 6
- residual: bfloat16 [8192, 2048], P('dp'), may hold values from -6 to 6
- out_weight: bfloat16 [1024, 2048], P(('section', 'mp')), may hold values from -0.1875 to 0.1875
- moe_gain: float32 [2048], replicated, may hold values from 0.1 to 1.9
- w_gate: bfloat16 [64, 2048, 1408], P('dp', None, ('section', 'mp')), may hold values from -0.125 to 0.125
- w_up: bfloat16 [64, 2048, 1408], P('dp', None, ('section', 'mp')), may hold values from -0.125 to 0.125
- w_down: bfloat16 [64, 1408, 2048], P('dp', ('section', 'mp')), may hold values from -0.15625 to 0.15625
- seg_ids: int32 [64, 1, 128], P('dp'), may hold values from 0 to 3, never falling along the last dimension, each value on 1 to 64 neighbouring positions
- prefix_blocks: int32 [64, 1, 4], P('dp'), may hold values from 1 to 32, 64 in all within a row
- owners: int32 [64, 1, 64, 1], replicated, may hold values from 0 to 63; in each aligned block of 64 rows (0 to 63, 64 to 127, ..., all dimensions but the last counted through in order) at most 3 rows name the same one
- slot_ids: int32 [64, 1, 64], replicated, may hold values from 0 to 63
- expert_ids: int32 [8192, 4], P('dp'), may hold values from 0 to 63, all different within a row; in each aligned block of 16 rows (0 to 15, 16 to 31, ...) at most 2 rows name the same one
- gate_weights: float32 [8192, 4], P('dp'), may hold values from 0.05 to 0.5
Outputs:
- layer_out: bfloat16 [8192, 2048], P('dp', ('section', 'mp'))
Inputs may be any that keep to these rules, and one draw needn't show every extreme that they name: seg_ids[g, m] never falls along the tokens; each of the 4 requests has 1 to 64 tokens, one exactly 64. `prefix_blocks`: the 4 counts of each (g, m) sum to 64, one of them is 32. `owners`: in each block table of 64 entries no owner appears more than 3 times, and some owner appears exactly 3 times in some table. `expert_ids`: each token names 4 different experts; in each aligned block of 16 tokens no expert is named by more than 2 tokens, a bound that some block reaches.
All inputs are finite; a program needn't handle non-finite values.
Results may differ from a plain program's by a relative error of at most 0.009.
Values may be sent and summed in bfloat16 or wider, within the bound.
No kernel may reach another device: no remote copies, remote signals or barrier semaphores. Data moves between devices by JAX's collectives and lax.ppermute only.
A program may use at most 64 MiB of HBM per device.

v0:
```python
import math

import jax
import jax.numpy as jnp
from jax import lax
from jax.sharding import PartitionSpec as P

HEAD_DIM = 128
TOPK = 4
PREF = 64
BLK = 8


def normalize(hidden, gain):
    square = jnp.mean(hidden * hidden, axis=-1, keepdims=True)
    return (hidden * lax.rsqrt(square + 1e-06) * gain).astype(jnp.bfloat16)


def expert_rows(inputs, w_gate, w_up, w_down):
    model_width = inputs.shape[-1]
    flat_rows = inputs.reshape(-1, model_width)
    gate_rows = jnp.dot(flat_rows, w_gate[0], preferred_element_type=jnp.float32)
    up_rows = jnp.dot(flat_rows, w_up[0], preferred_element_type=jnp.float32)
    hidden = (jax.nn.silu(gate_rows) * up_rows).astype(jnp.bfloat16)
    result = jnp.dot(hidden, w_down[0], preferred_element_type=jnp.float32).astype(jnp.bfloat16)
    return result.reshape(inputs.shape[:-1] + (result.shape[-1],))


def slot_table(pair_ids, pair_slots, experts, capacity):
    pair_count = pair_ids.shape[0]
    expert_match = pair_ids[None, None, :] == jnp.arange(experts, dtype=jnp.int32)[:, None, None]
    slot_match = pair_slots[None, None, :] == jnp.arange(capacity, dtype=jnp.int32)[None, :, None]
    pair_match = expert_match & slot_match
    token_of = jnp.arange(pair_count, dtype=jnp.int32) // TOPK
    source = jnp.sum(jnp.where(pair_match, token_of[None, None, :], 0), axis=2)
    filled = jnp.any(pair_match, axis=2)
    return (source, filled)


def dispatch_rows(normed, source, filled):
    gathered = jnp.take(normed, source.reshape(-1), axis=0).reshape(
        source.shape + (normed.shape[-1],)
    )
    return jnp.where(filled[:, :, None], gathered, jnp.zeros_like(gathered))


def local(
    qkv,
    kv_cache,
    residual,
    out_weight,
    moe_gain,
    w_gate,
    w_up,
    w_down,
    seg_ids,
    prefix_blocks,
    owners,
    slot_ids,
    expert_ids,
    gate_weights,
):
    groups = lax.axis_size("dp")
    shards = lax.axis_size("section") * lax.axis_size("mp")
    group_index = lax.axis_index("dp")
    shard_index = lax.axis_index("section") * lax.axis_size("mp") + lax.axis_index("mp")
    mb_rows = seg_ids.shape[2]
    quarter_rows = mb_rows // shards
    model_width = residual.shape[1]
    part_cols = model_width // shards
    head_cols = out_weight.shape[0]
    heads_local = head_cols // HEAD_DIM
    cache_cols = kv_cache.shape[2]
    quarter_cap = min(quarter_rows, max(2, 2 * quarter_rows * TOPK // groups))
    capacity = shards * quarter_cap
    owner_cap = max(3, 3 * PREF // groups)
    score_scale = 1.0 / math.sqrt(HEAD_DIM)
    own_table = owners[:, 0, :, 0]
    slot_table_m = slot_ids[:, 0, :]
    owned_here = own_table == group_index
    local_order = jnp.cumsum(owned_here.astype(jnp.int32), axis=1) - 1
    wanted = owned_here[:, None, :] & (
        local_order[:, None, :] == jnp.arange(owner_cap, dtype=jnp.int32)[None, :, None]
    )
    slot_pick = jnp.sum(jnp.where(wanted, slot_table_m[:, None, :], 0), axis=2)
    filled = jnp.any(wanted, axis=2)
    chosen = jnp.take(kv_cache, slot_pick.reshape(-1), axis=0).reshape(
        groups, owner_cap, BLK, cache_cols
    )
    chosen = jnp.where(filled[:, :, None, None], chosen, jnp.zeros_like(chosen))
    arrived = lax.all_to_all(chosen, "dp", split_axis=0, concat_axis=0, tiled=True)
    my_owner = lax.dynamic_index_in_dim(own_table, group_index, 0, keepdims=False)
    block_index = jnp.arange(PREF, dtype=jnp.int32)
    earlier = (my_owner[None, :] == my_owner[:, None]) & (
        block_index[None, :] < block_index[:, None]
    )
    my_rank = jnp.sum(earlier.astype(jnp.int32), axis=1)
    where_from = my_owner * owner_cap + my_rank
    prefix = jnp.take(arrived.reshape(groups * owner_cap, BLK, cache_cols), where_from, axis=0)
    prefix = prefix.reshape(PREF * BLK, heads_local, 2, HEAD_DIM)
    tokens = qkv
    tokens = tokens.reshape(mb_rows, heads_local, 3, HEAD_DIM)
    query_rows = tokens[:, :, 0]
    key_rows = jnp.concatenate([prefix[:, :, 0], tokens[:, :, 1]], axis=0)
    value_rows = jnp.concatenate([prefix[:, :, 1], tokens[:, :, 2]], axis=0)
    segments = seg_ids[0, 0]
    block_ends = jnp.cumsum(prefix_blocks[0, 0])
    block_seg = jnp.sum((block_ends[None, :] <= block_index[:, None]).astype(jnp.int32), axis=1)
    prefix_seg = jnp.repeat(block_seg, BLK)
    position = jnp.arange(mb_rows, dtype=jnp.int32)
    same_prefix = prefix_seg[None, :] == segments[:, None]
    same_new = (segments[None, :] == segments[:, None]) & (position[None, :] <= position[:, None])
    visible = jnp.concatenate([same_prefix, same_new], axis=1)
    scores = (
        jnp.einsum("qhd,khd->hqk", query_rows, key_rows, preferred_element_type=jnp.float32)
        * score_scale
    )
    scores = jnp.where(visible[None], scores, -jnp.inf)
    row_max = jnp.max(scores, axis=2, keepdims=True)
    weights = jnp.exp(scores - row_max)
    attention = (weights / jnp.sum(weights, axis=2, keepdims=True)).astype(jnp.bfloat16)
    combined = jnp.einsum("hqk,khd->qhd", attention, value_rows, preferred_element_type=jnp.float32)
    attended_now = combined.astype(jnp.bfloat16).reshape(mb_rows, head_cols)
    stream = residual.astype(jnp.float32)
    projected = jnp.dot(attended_now, out_weight, preferred_element_type=jnp.float32)
    quarter_ids = expert_ids.reshape(shards, quarter_rows * TOPK)
    one_hot = (
        quarter_ids[:, :, None] == jnp.arange(groups, dtype=jnp.int32)[None, None, :]
    ).astype(jnp.int32)
    quarter_rank = jnp.sum((jnp.cumsum(one_hot, axis=1) - one_hot) * one_hot, axis=2)
    flat_ids = expert_ids.reshape(-1)
    flat_slot = (quarter_rank + jnp.arange(shards, dtype=jnp.int32)[:, None] * quarter_cap).reshape(
        -1
    )
    mixed_in = stream + lax.psum(projected, ("section", "mp"))
    normed = normalize(mixed_in, moe_gain)
    source, filled = slot_table(flat_ids, flat_slot, groups, capacity)
    outgoing = dispatch_rows(normed, source, filled)
    incoming = lax.all_to_all(outgoing, "dp", split_axis=0, concat_axis=0, tiled=True)
    produced = expert_rows(incoming, w_gate, w_up, w_down)
    returned = lax.all_to_all(produced, "dp", split_axis=0, concat_axis=0, tiled=True)
    position = flat_ids * capacity + flat_slot
    picked = jnp.take(returned.reshape(groups * capacity, model_width), position, axis=0)
    picked = picked.reshape(mb_rows, TOPK, model_width)
    weighted = jnp.einsum("tk,tkd->td", gate_weights, picked.astype(jnp.float32))
    moe_full = lax.psum(weighted.astype(jnp.bfloat16), ("section", "mp")).astype(jnp.float32)
    finished = (mixed_in + moe_full).astype(jnp.bfloat16).reshape(mb_rows, shards, part_cols)
    return lax.dynamic_index_in_dim(finished, shard_index, 1, keepdims=False)


def solution(mesh):
    return jax.shard_map(
        local,
        mesh=mesh,
        in_specs=(
            P("dp", ("section", "mp")),
            P("dp", None, ("section", "mp")),
            P("dp", None),
            P(("section", "mp"), None),
            P(),
            P("dp", None, ("section", "mp")),
            P("dp", None, ("section", "mp")),
            P("dp", ("section", "mp"), None),
            P("dp", None, None),
            P("dp", None, None),
            P(),
            P(),
            P("dp", None),
            P("dp", None),
        ),
        out_specs=P("dp", ("section", "mp")),
        check_vma=False,
    )
```

profile of v0, /device:TPU:1, one launch (start us, length us, event | category | flops | bytes accessed | tf_op | source)
XLA Modules:
  0.0 660.9 jit_solution(7814979342064895918)
XLA Ops:
  6.6 0.9 broadcast_compare_fusion.1
  7.7 0.9 select_reduce_fusion
  9.2 1.8 gather_fusion
  11.0 1.3 select_select_fusion.1
  12.4 19.3 %all-to-all-start = ((bf16[64,3,8,256]{3,2,1,0:T(8,128)(2,1)}), bf16[64,3,8,256]{3,2,1,0:T(8,128)(2,1)S(1)}, u32[]{:S(2)}, u32[]{:S(2)}) async-start(bf16[64,3,8,256]{3,2,1,0:T(8,128)(2,1)} %select_select_fusion.1), calls=%async_computation | async-start | bytes 1572864 | tf_op jit(solution)/shard_map/all_to_all | solution.py:91
  32.0 0.7 fusion.43
  32.9 0.7 compare_and_fusion.3
  34.6 1.4 fusion.53
  36.3 1.2 fusion
  37.6 0.7 fusion.42
  38.5 33.9 %all-to-all-done = bf16[64,3,8,256]{3,2,1,0:T(8,128)(2,1)S(1)} async-done(((bf16[64,3,8,256]{3,2,1,0:T(8,128)(2,1)}), bf16[64,3,8,256]{3,2,1,0:T(8,128)(2,1)S(1)}, u32[]{:S(2)}, u32[]{:S(2)}) %all-to-all-start) | async-done | bytes 786464 | tf_op jit(solution)/shard_map/all_to_all | solution.py:91
  73.0 1.8 broadcast_select_fusion
  75.6 1.5 fusion.8
  77.1 1.2 and_reduce_fusion
  78.3 70.4 %all-reduce.3.cloned.1.call-done = f32[128,2048]{1,0:T(8,128)} async-done(((f32[128,2048]{1,0:T(8,128)}), f32[128,2048]{1,0:T(8,128)}) %all-reduce.3.cloned.1.call-update) | async-done | bytes 1048592 | tf_op jit(solution)/shard_map/psum | solution.py:135
  148.7 1.4 multiply_reduce_fusion
  150.2 1.4 multiply_convert_fusion
  151.6 6.0 gather_fusion.2
  157.6 2.6 select_select_fusion
  160.2 198.9 %all_to_all.15 = bf16[64,16,2048]{2,1,0:T(8,128)(2,1)S(1)} all-to-all(bf16[64,16,2048]{2,1,0:T(8,128)(2,1)S(1)} %select_select_fusion), channel_id=1, replica_groups=mesh['section'=2,'dp'=64,'mp'=4] {'dp'}, dimensions={0} | all-to-all | bytes 8388608 | tf_op jit(solution)/shard_map/all_to_all | solution.py:139
  359.1 2.0 copy-done.3
  361.1 1.5 fusion.14
  362.6 6.8 %convolution_convert_fusion = bf16[1024,2048]{1,0:T(8,128)(2,1)} fusion(bf16[1024,2048]{1,0:T(8,128)(2,1)} %bitcast.88, bf16[1,176,2048]{2,1,0:T(8,128)(2,1)S(1)} %copy-done, bf16[1,2048,176]{1,2,0:T(8,128)(2,1)S(1)} %copy-done.11, f32[1024,176]{0,1:T(8,128)S(1)} %fusion.14), kind=kOutput, calls=%fused_computation.5 | convolution fusion | flops 1479573504 | bytes 10551296 | tf_op jit(solution)/shard_map/dot_general | solution.py:25
  369.5 10.3 %all-to-all-start.2 = ((bf16[64,16,2048]{2,1,0:T(8,128)(2,1)}), bf16[64,16,2048]{2,1,0:T(8,128)(2,1)}, u32[]{:S(2)}, u32[]{:S(2)}) async-start(bf16[64,16,2048]{2,1,0:T(8,128)(2,1)} %bitcast.86), calls=%async_computation.2 | async-start | bytes 8388608 | tf_op jit(solution)/shard_map/all_to_all | solution.py:141
  380.9 181.4 %all-to-all-done.2 = bf16[64,16,2048]{2,1,0:T(8,128)(2,1)} async-done(((bf16[64,16,2048]{2,1,0:T(8,128)(2,1)}), bf16[64,16,2048]{2,1,0:T(8,128)(2,1)}, u32[]{:S(2)}, u32[]{:S(2)}) %all-to-all-start.2) | async-done | bytes 4194336 | tf_op jit(solution)/shard_map/all_to_all | solution.py:141
  562.2 7.1 %gather_fusion.3 = bf16[512,2048]{1,0:T(8,128)(2,1)S(1)} fusion(bf16[1024,2048]{1,0:T(8,128)(2,1)} %bitcast.28, s32[1024]{0:T(1024)S(1)} %pad_clamp_fusion), kind=kCustom, calls=%fused_computation.3 | custom fusion | bytes 4196352 | tf_op jit(solution)/shard_map/jit(_take)/gather | solution.py:143
  569.4 2.2 gather.31
  571.6 3.0 fusion.1
  574.6 1.1 copy.100
  575.8 76.2 %all-reduce.5.cloned.1.call-done = bf16[128,2048]{1,0:T(8,128)(2,1)} async-done(((bf16[128,2048]{1,0:T(8,128)(2,1)}), bf16[128,2048]{1,0:T(8,128)(2,1)}) %all-reduce.5.cloned.1.call-update) | async-done | bytes 524304 | tf_op jit(solution)/shard_map/psum | solution.py:146
  652.0 1.2 add_convert_fusion
  653.5 0.6 copy.101
  (91 shorter events, 5.8 us)
Async XLA Ops:
  6.5 356.1 %copy-start = (bf16[1,176,2048]{2,1,0:T(8,128)(2,1)S(1)}, bf16[1,176,2048]{2,1,0:T(8,128)(2,1)}, u32[]{:S(2)}) copy-start(bf16[1,176,2048]{2,1,0:T(8,128)(2,1)} %param.21) | copy-start | bytes 2162692
  6.5 25.2 %copy-start.6 = (s32[128,4]{0,1:T(4,128)S(1)}, s32[128,4]{0,1:T(4,128)}, u32[]{:S(2)}) copy-start(s32[128,4]{0,1:T(4,128)} %param.26) | copy-start | bytes 6148
  6.5 27.2 %copy-start.5 = (bf16[128,384]{1,0:T(8,128)(2,1)S(1)}, bf16[128,384]{1,0:T(8,128)(2,1)}, u32[]{:S(2)}) copy-start(bf16[128,384]{1,0:T(8,128)(2,1)} %param.14) | copy-start | bytes 294916
  6.5 27.4 %copy-start.12 = (s32[1,1,4]{2,1,0:T(1,128)S(1)}, s32[1,1,4]{2,1,0:T(1,128)}, u32[]{:S(2)}) copy-start(s32[1,1,4]{2,1,0:T(1,128)} %param.23) | copy-start | bytes 52
  6.5 31.7 %copy-start.8 = (s32[1,1,128]{2,1,0:T(1,128)S(1)}, s32[1,1,128]{2,1,0:T(1,128)}, u32[]{:S(2)}) copy-start(s32[1,1,128]{2,1,0:T(1,128)} %param.22) | copy-start | bytes 1540
  11.0 64.5 %copy-start.4 = (bf16[128,2048]{1,0:T(8,128)(2,1)S(1)}, bf16[128,2048]{1,0:T(8,128)(2,1)}, u32[]{:S(2)}) copy-start(bf16[128,2048]{1,0:T(8,128)(2,1)} %param.17) | copy-start | bytes 1572868
  12.4 60.0 %all-to-all-start = ((bf16[64,3,8,256]{3,2,1,0:T(8,128)(2,1)}), bf16[64,3,8,256]{3,2,1,0:T(8,128)(2,1)S(1)}, u32[]{:S(2)}, u32[]{:S(2)}) async-start(bf16[64,3,8,256]{3,2,1,0:T(8,128)(2,1)} %select_select_fusion.1), calls=%async_computation | async-start | bytes 1572864 | tf_op jit(solution)/shard_map/all_to_all | solution.py:91
  31.6 117.1 %all-reduce.3.cloned.1.call-start = ((), (), s32[]{:S(2)}) async-start(), calls=%async_computation.3 | async-start | bytes 2097152 | tf_op jit(solution)/shard_map/psum | solution.py:135
  34.3 114.4 %copy-start.2 = (bf16[128,2048]{1,0:T(8,128)(2,1)S(1)}, bf16[128,2048]{1,0:T(8,128)(2,1)}, u32[]{:S(2)}) copy-start(bf16[128,2048]{1,0:T(8,128)(2,1)} %param.16) | copy-start | bytes 1572868
  73.0 77.2 %copy-start.7 = (f32[2048]{0:T(1024)S(1)}, f32[2048]{0:T(1024)}, u32[]{:S(2)}) copy-start(f32[2048]{0:T(1024)} %param.18) | copy-start | bytes 24580
  160.2 200.9 %copy-start.10 = (bf16[1,2048,176]{1,2,0:T(8,128)(2,1)S(1)}, bf16[1,2048,176]{1,2,0:T(8,128)(2,1)}, u32[]{:S(2)}) copy-start(bf16[1,2048,176]{1,2,0:T(8,128)(2,1)} %param.19) | copy-start | bytes 2162692
  359.1 2.0 copy-start.3
  359.1 3.5 copy-start.11
  369.5 11.2 %copy-start.9 = (f32[128,4]{0,1:T(4,128)S(1)}, f32[128,4]{0,1:T(4,128)}, u32[]{:S(2)}) copy-start(f32[128,4]{0,1:T(4,128)} %param.27) | copy-start | bytes 6148
  369.5 192.8 %all-to-all-start.2 = ((bf16[64,16,2048]{2,1,0:T(8,128)(2,1)}), bf16[64,16,2048]{2,1,0:T(8,128)(2,1)}, u32[]{:S(2)}, u32[]{:S(2)}) async-start(bf16[64,16,2048]{2,1,0:T(8,128)(2,1)} %bitcast.86), calls=%async_computation.2 | async-start | bytes 8388608 | tf_op jit(solution)/shard_map/all_to_all | solution.py:141
  379.8 272.1 %all-reduce.5.cloned.1.call-start = ((), (), s32[]{:S(2)}) async-start(), calls=%async_computation.4 | async-start | bytes 1048576 | tf_op jit(solution)/shard_map/psum | solution.py:146
  571.6 80.4 %copy-start.1 = (f32[128,2048]{1,0:T(8,128)S(1)}, f32[128,2048]{1,0:T(8,128)}, u32[]{:S(2)}) copy-start(f32[128,2048]{1,0:T(8,128)} %all-reduce.3.cloned.1.call-done) | copy-start | bytes 3145732
Sparse Core Ops, SparseCore 0:
  77.2 71.4 all-reduce.2
  575.9 76.0 all-reduce.4
where the time goes:
time: 662 us; the launch traced here: 661 us
  waiting for transfers between devices  362 us (55%)
  blocking collectives  199 us (30%)
  starting transfers between devices  29.7 us (4%)
  local copies, waits for them, and re-layouts  25.6 us (4%)
  other arithmetic  17.9 us (3%)
  between operations  13.8 us (2%)
  matrix products  13.2 us (2%)
    all_to_all x1, blocking collectives, local(): lax.all_to_all(outgoing, 'dp', split_axis=0, concat_axis=0, tiled=True)  199 us
    all_to_all x1, waiting for transfers between devices, local(): lax.all_to_all(produced, 'dp', split_axis=0, concat_axis=0, tiled=True)  181 us
    psum x1, waiting for transfers between devices, local(): lax.psum(weighted.astype(jnp.bfloat16), ('section', 'mp'))  76.2 us
    psum x1, waiting for transfers between devices, local(): mixed_in = stream + lax.psum(projected, ('section', 'mp'))  70.4 us
    all_to_all x1, waiting for transfers between devices, local(): lax.all_to_all(chosen, 'dp', split_axis=0, concat_axis=0, tiled=True)  33.9 us
    all_to_all x1, starting transfers between devices, local(): lax.all_to_all(chosen, 'dp', split_axis=0, concat_axis=0, tiled=True)  19.3 us
  transfers between devices with their start and end apart: 4, of which 4 were waited for; matrix products, arithmetic and copies ran while one was open for 1% of the time, Pallas kernels for 0%

commit v1 on v0

v1 whole, which is shorter than its diff:
```python
import math

import jax
import jax.numpy as jnp
from jax import lax
from jax.experimental import pallas as pl
from jax.experimental.pallas import tpu as pltpu
from jax.sharding import PartitionSpec as P

HEAD_DIM = 128
TOPK = 4
PREF = 64
BLK = 8
OWN_CAP = 3
CAPQ = 2
SPLIT = ("section", "mp")


def nt_dot(a, b):
    return lax.dot_general(a, b, (((1,), (1,)), ((), ())), preferred_element_type=jnp.float32)


def attend_kernel(qkv_ref, prefix_ref, key_seg_ref, seg_row_ref, seg_col_ref, weight_ref, out_ref):
    rows = qkv_ref.shape[0]
    query = qkv_ref[:, :HEAD_DIM]
    scale = 1.0 / math.sqrt(HEAD_DIM)
    old = nt_dot(query, prefix_ref[:, :HEAD_DIM]) * scale
    new = nt_dot(query, qkv_ref[:, HEAD_DIM : 2 * HEAD_DIM]) * scale
    seg = seg_col_ref[...]
    earlier = lax.broadcasted_iota(jnp.int32, (rows, rows), 1) <= lax.broadcasted_iota(
        jnp.int32, (rows, rows), 0
    )
    old = jnp.where(key_seg_ref[...] == seg, old, -jnp.inf)
    new = jnp.where((seg_row_ref[...] == seg) & earlier, new, -jnp.inf)
    top = jnp.maximum(
        jnp.max(old, axis=1, keepdims=True), jnp.max(new, axis=1, keepdims=True)
    )
    old = jnp.exp(old - top)
    new = jnp.exp(new - top)
    total = jnp.sum(old, axis=1, keepdims=True) + jnp.sum(new, axis=1, keepdims=True)
    old = (old / total).astype(jnp.bfloat16)
    new = (new / total).astype(jnp.bfloat16)
    attended = jnp.dot(
        old, prefix_ref[:, HEAD_DIM:], preferred_element_type=jnp.float32
    ) + jnp.dot(new, qkv_ref[:, 2 * HEAD_DIM :], preferred_element_type=jnp.float32)
    out_ref[...] = jnp.dot(
        attended.astype(jnp.bfloat16), weight_ref[...], preferred_element_type=jnp.float32
    ).astype(out_ref.dtype)


def norm_kernel(parts_ref, residual_ref, gain_ref, pick_ref, mixed_ref, out_ref):
    mixed = residual_ref[...].astype(jnp.float32)
    projected = parts_ref[0].astype(jnp.float32)
    for i in range(1, parts_ref.shape[0]):
        projected = projected + parts_ref[i].astype(jnp.float32)
    mixed = mixed + projected
    mixed_ref[...] = mixed
    square = jnp.mean(mixed * mixed, axis=1, keepdims=True)
    normed = (mixed * lax.rsqrt(square + 1e-06) * gain_ref[...]).astype(jnp.bfloat16)
    out_ref[...] = jnp.dot(pick_ref[...], normed, preferred_element_type=jnp.float32).astype(
        jnp.bfloat16
    )


def combine_kernel(rows_ref, gate_ref, mixed_ref, out_ref):
    gate = gate_ref[...]
    high = gate.astype(jnp.bfloat16)
    low = (gate - high.astype(jnp.float32)).astype(jnp.bfloat16)
    rows = rows_ref[...]
    total = jnp.dot(high, rows, preferred_element_type=jnp.float32)
    total = total + jnp.dot(low, rows, preferred_element_type=jnp.float32)
    total = (total + mixed_ref[...]).astype(jnp.bfloat16)
    cols = out_ref.shape[2]
    for i in range(out_ref.shape[0]):
        out_ref[i] = total[:, i * cols : (i + 1) * cols]


def local(
    qkv,
    kv_cache,
    residual,
    out_weight,
    moe_gain,
    w_gate,
    w_up,
    w_down,
    seg_ids,
    prefix_blocks,
    owners,
    slot_ids,
    expert_ids,
    gate_weights,
):
    groups = lax.axis_size("dp")
    shards = lax.axis_size("section") * lax.axis_size("mp")
    group = lax.axis_index("dp")
    shard = lax.axis_index("section") * lax.axis_size("mp") + lax.axis_index("mp")
    rows = seg_ids.shape[2]
    block = rows // shards
    width = residual.shape[1]
    cols = width // shards
    slots = groups * CAPQ

    table = owners[:, 0, :, 0]
    owned = table == group
    order = jnp.cumsum(owned.astype(jnp.int32), axis=1) - 1
    wanted = owned[:, None, :] & (
        order[:, None, :] == jnp.arange(OWN_CAP, dtype=jnp.int32)[None, :, None]
    )
    pick = jnp.sum(jnp.where(wanted, slot_ids[:, 0, :][:, None, :], 0), axis=2)
    chosen = kv_cache.at[pick.reshape(-1)].get(mode="promise_in_bounds")
    chosen = chosen.reshape(groups, OWN_CAP, BLK, kv_cache.shape[2])
    arrived = lax.all_to_all(chosen, "dp", split_axis=0, concat_axis=0, tiled=True)

    full_gate = lax.all_gather(w_gate[0].T, SPLIT, axis=0, tiled=True)
    full_up = lax.all_gather(w_up[0].T, SPLIT, axis=0, tiled=True)
    full_down = lax.all_gather(w_down[0], SPLIT, axis=0, tiled=True)

    mine = lax.dynamic_index_in_dim(table, group, 0, keepdims=False)
    index = jnp.arange(PREF, dtype=jnp.int32)
    before = (mine[None, :] == mine[:, None]) & (index[None, :] < index[:, None])
    place = mine * OWN_CAP + jnp.sum(before.astype(jnp.int32), axis=1)
    ends = jnp.cumsum(prefix_blocks[0, 0])
    block_seg = jnp.sum((ends[None, :] <= index[:, None]).astype(jnp.int32), axis=1)
    key_slot = jnp.arange(groups * OWN_CAP * BLK, dtype=jnp.int32) // BLK
    key_seg = (
        jnp.sum(jnp.where(place[:, None] == key_slot[None, :], block_seg[:, None] + 1, 0), axis=0)
        - 1
    )[None, :]
    segments = seg_ids[0, 0]

    first = shard * block
    ids = lax.dynamic_slice_in_dim(expert_ids, first, block, 0)
    gates = lax.dynamic_slice_in_dim(gate_weights, first, block, 0)
    flat = ids.reshape(-1)
    pair = jnp.arange(block * TOPK, dtype=jnp.int32)
    same = (flat[None, :] == flat[:, None]) & (pair[None, :] < pair[:, None])
    slot = (flat * CAPQ + jnp.sum(same.astype(jnp.int32), axis=1)).reshape(block, TOPK)
    slot_index = jnp.arange(slots, dtype=jnp.int32)
    hit = slot[:, :, None] == slot_index[None, None, :]
    gate_matrix = jnp.sum(jnp.where(hit, gates[:, :, None], 0.0), axis=1)
    pick_matrix = jnp.any(slot.T[None, :, :] == slot_index[:, None, None], axis=1).astype(
        jnp.bfloat16
    )
    my_residual = lax.dynamic_slice_in_dim(residual, first, block, 0)

    projected = pl.pallas_call(
        attend_kernel,
        out_shape=jax.ShapeDtypeStruct((rows, width), jnp.bfloat16),
        name="attend",
    )(
        qkv,
        arrived.reshape(-1, kv_cache.shape[2]),
        key_seg,
        segments[None, :],
        segments[:, None],
        out_weight,
    )
    parts = lax.all_to_all(
        projected.reshape(shards, block, width), SPLIT, split_axis=0, concat_axis=0, tiled=True
    )
    mixed, outgoing = pl.pallas_call(
        norm_kernel,
        out_shape=(
            jax.ShapeDtypeStruct((block, width), jnp.float32),
            jax.ShapeDtypeStruct((slots, width), jnp.bfloat16),
        ),
        name="norm",
    )(parts, my_residual, moe_gain[None, :], pick_matrix)
    incoming = lax.all_to_all(
        outgoing.reshape(groups, CAPQ, width), "dp", split_axis=0, concat_axis=0, tiled=True
    ).reshape(slots, width)

    hidden = (jax.nn.silu(nt_dot(incoming, full_gate)) * nt_dot(incoming, full_up)).astype(
        jnp.bfloat16
    )
    produced = jnp.dot(hidden, full_down, preferred_element_type=jnp.float32).astype(jnp.bfloat16)
    returned = lax.all_to_all(
        produced.reshape(groups, CAPQ, width), "dp", split_axis=0, concat_axis=0, tiled=True
    ).reshape(slots, width)
    finished = pl.pallas_call(
        combine_kernel,
        out_shape=jax.ShapeDtypeStruct((shards, block, cols), jnp.bfloat16),
        name="combine",
    )(returned, gate_matrix, mixed)
    result = lax.all_to_all(finished, SPLIT, split_axis=0, concat_axis=0, tiled=True)
    return result.reshape(rows, cols)


def solution(mesh):
    return jax.shard_map(
        local,
        mesh=mesh,
        in_specs=(
            P("dp", ("section", "mp")),
            P("dp", None, ("section", "mp")),
            P("dp", None),
            P(("section", "mp"), None),
            P(),
            P("dp", None, ("section", "mp")),
            P("dp", None, ("section", "mp")),
            P("dp", ("section", "mp"), None),
            P("dp", None, None),
            P("dp", None, None),
            P(),
            P(),
            P("dp", None),
            P("dp", None),
        ),
        out_specs=P("dp", ("section", "mp")),
        check_vma=False,
    )
```

time: 662 us -> 236 us (0.36)
  waiting for transfers between devices: 362 us -> 93.8 us
  blocking collectives: 199 us -> 48.4 us
  other arithmetic: 17.9 us -> 4.14 us
  starting transfers between devices: 29.7 us -> 43.4 us
  local copies, waits for them, and re-layouts: 25.6 us -> 12.9 us
  Pallas kernels: 0 us -> 7.56 us
    all_to_all x1 -> x2, blocking collectives: 199 us -> 48.4 us  [the longest x1 37.6 us: local(): lax.all_to_all(outgoing.reshape(groups, CAPQ, width), 'dp', split_axis=0,...]
    psum x2 -> x0, waiting for transfers between devices: 147 us -> none  [the longest x1 76.2 us: local(): lax.psum(weighted.astype(jnp.bfloat16), ('section', 'mp'))]
    all_to_all x1 -> x2, waiting for transfers between devices: 181 us -> 41.6 us  [the longest x1 30.3 us: local(): lax.all_to_all(produced.reshape(groups, CAPQ, width), 'dp', split_axis=0,...]
    gather x6 -> x1, local copies, waits for them, and re-layouts: 17.8 us -> 2.67 us  [local(): chosen = kv_cache.at[pick.reshape(-1)].get(mode='promise_in_bounds')]
    all_to_all x1 -> x2, starting transfers between devices: 10.3 us -> 24 us  [the longest x1 15.4 us: local(): lax.all_to_all(produced.reshape(groups, CAPQ, width), 'dp', split_axis=0,...]
    all_gather x0 -> x3, waiting for transfers between devices: none -> 13.3 us  [the longest x1 13.2 us: local(): full_down = lax.all_gather(w_down[0], SPLIT, axis=0, tiled=True)]
    pallas_call x0 -> x3, Pallas kernels: none -> 7.56 us  [the longest x1 3.25 us: local(): pl.pallas_call(attend_kernel, out_shape=jax.ShapeDtypeStruct((rows, width...]
  transfers between devices with their start and end apart: 4 -> 6, of which waited for: 4 -> 4; matrix products, arithmetic and copies ran while one was open for 1% -> 7% of each run, Pallas kernels for 0% -> 2%
where the time goes in v1:
time: 236 us
  waiting for transfers between devices  93.8 us (40%)
  blocking collectives  48.4 us (21%)
  starting transfers between devices  43.4 us (18%)
  between operations  13.3 us (6%)
  local copies, waits for them, and re-layouts  12.9 us (5%)
  matrix products  12.1 us (5%)
  Pallas kernels  7.56 us (3%)
  other arithmetic  4.14 us (2%)
    all_to_all x1, blocking collectives, local(): lax.all_to_all(outgoing.reshape(groups, CAPQ, width), 'dp', split_axis=0,...  37.6 us
    all_to_all x1, waiting for transfers between devices, local(): lax.all_to_all(chosen, 'dp', split_axis=0, concat_axis=0, tiled=True)  36.9 us
    all_to_all x1, waiting for transfers between devices, local(): lax.all_to_all(produced.reshape(groups, CAPQ, width), 'dp', split_axis=0,...  30.3 us
    all_to_all x1, starting transfers between devices, local(): lax.all_to_all(chosen, 'dp', split_axis=0, concat_axis=0, tiled=True)  19.3 us
    all_to_all x1, starting transfers between devices, local(): lax.all_to_all(produced.reshape(groups, CAPQ, width), 'dp', split_axis=0,...  15.4 us
    all_gather x1, waiting for transfers between devices, local(): full_down = lax.all_gather(w_down[0], SPLIT, axis=0, tiled=True)  13.2 us
    all_to_all x1, waiting for transfers between devices, local(): lax.all_to_all(projected.reshape(shards, block, width), SPLIT, split_axis...  11.3 us
    all_to_all x1, blocking collectives, local(): lax.all_to_all(finished, SPLIT, split_axis=0, concat_axis=0, tiled=True)  10.9 us
  transfers between devices with their start and end apart: 6, of which 4 were waited for; matrix products, arithmetic and copies ran while one was open for 7% of the time, Pallas kernels for 2%

profile of v1, /device:TPU:1, one launch (start us, length us, event | category | flops | bytes accessed | tf_op | source)
XLA Modules:
  0.0 235.6 jit_solution(1663629467181217203)
XLA Ops:
  6.6 0.7 all-gather.5.cloned.1.call-update
  7.3 0.7 all-gather.7.cloned.1.call-update
  8.1 0.7 all-gather.9.cloned.1.call-update
  8.8 0.8 broadcast_compare_fusion
  9.8 0.9 select_reduce_fusion.1
  11.0 2.7 %gather_fusion = bf16[192,8,256]{2,1,0:T(8,128)(2,1)} fusion(bf16[64,8,256]{2,1,0:T(8,128)(2,1)} %param.15, s32[1024]{0:T(1024)S(1)} %pad_clamp_fusion), kind=kCustom, calls=%fused_computation | custom fusion | bytes 1573632 | tf_op jit(solution)/shard_map/gather | solution.py:111
  13.7 19.3 %all-to-all-start = ((bf16[64,3,8,256]{3,2,1,0:T(8,128)(2,1)}), bf16[64,3,8,256]{3,2,1,0:T(8,128)(2,1)S(1)}, u32[]{:S(2)}, u32[]{:S(2)}) async-start(bf16[64,3,8,256]{3,2,1,0:T(8,128)(2,1)} %bitcast.2), calls=%async_computation | async-start | bytes 1572864 | tf_op jit(solution)/shard_map/all_to_all | solution.py:113
  33.1 0.7 fusion.14
  34.1 0.7 multiply_add_fusion.1
  35.5 0.7 copy.30.seg_col_ref
  36.7 36.9 %all-to-all-done = bf16[64,3,8,256]{3,2,1,0:T(8,128)(2,1)S(1)} async-done(((bf16[64,3,8,256]{3,2,1,0:T(8,128)(2,1)}), bf16[64,3,8,256]{3,2,1,0:T(8,128)(2,1)S(1)}, u32[]{:S(2)}, u32[]{:S(2)}) %all-to-all-start) | async-done | bytes 786464 | tf_op jit(solution)/shard_map/all_to_all | solution.py:113
  73.6 0.9 copy-done.1
  74.5 3.3 %attend.1 = bf16[128,2048]{1,0:T(8,128)(2,1)} custom-call(bf16[128,384]{1,0:T(8,128)(2,1)} %qkv_ref.1, bf16[1536,256]{1,0:T(8,128)(2,1)} %bitcast.34, s32[1,1536]{1,0:T(1,128)} %sub.19.key_seg_ref, s32[1,128]{1,0:T(1,128)} %bitcast.43, s32[128,1]{1,0:T(8,128)} %copy.30.seg_col_ref, bf16[128,2048]{1,0:T(8,128)(2,1)} %weight_ref.1), custom_call_target="tpu_custom_call" | custom-call | tf_op jit(solution)/shard_map/attend/pallas_call | solution.py:147
  77.8 8.6 %all-to-all-start.1 = ((bf16[8,16,2048]{2,1,0:T(8,128)(2,1)}), bf16[8,16,2048]{2,1,0:T(8,128)(2,1)S(1)}, u32[]{:S(2)}, u32[]{:S(2)}) async-start(bf16[8,16,2048]{2,1,0:T(8,128)(2,1)} %bitcast.35), calls=%async_computation.1 | async-start | bytes 1048576 | tf_op jit(solution)/shard_map/all_to_all | solution.py:159
  86.6 0.7 copy.33.pick_ref
  87.3 0.6 constant_dynamic-slice_fusion.1.residual_ref
  87.9 11.3 %all-to-all-done.1.parts_ref = bf16[8,16,2048]{2,1,0:T(8,128)(2,1)S(1)} async-done(((bf16[8,16,2048]{2,1,0:T(8,128)(2,1)}), bf16[8,16,2048]{2,1,0:T(8,128)(2,1)S(1)}, u32[]{:S(2)}, u32[]{:S(2)}) %all-to-all-start.1) | async-done | bytes 524320 | tf_op jit(solution)/shard_map/all_to_all | solution.py:159
  99.3 0.8 copy-done.2
  100.1 2.3 norm.1
  102.4 1.4 reshape.157
  103.8 37.6 %all_to_all.25 = bf16[64,2,2048]{2,1,0:T(2,128)(2,1)S(1)} all-to-all(bf16[64,2,2048]{2,1,0:T(2,128)(2,1)S(1)} %reshape.157), channel_id=1, replica_groups=mesh['section'=2,'dp'=64,'mp'=4] {'dp'}, dimensions={0} | all-to-all | bytes 1048576 | tf_op jit(solution)/shard_map/all_to_all | solution.py:170
  141.6 4.7 %fusion.17 = f32[128,1408]{1,0:T(8,128)S(1)} fusion(bf16[128,2048]{1,0:T(8,128)(2,1)S(1)} %reshape.158, bf16[1408,2048]{1,0:T(8,128)(2,1)} %all-gather.5.cloned.1.call-done), kind=kOutput, calls=%fused_computation.45 | convolution fusion | flops 738197504 | bytes 7012352 | tf_op jit(solution)/shard_map/dot_general | solution.py:20
  146.3 13.2 %all-gather.9.cloned.1.call-done = bf16[1,1408,2048]{2,1,0:T(8,128)(2,1)} async-done(((bf16[1,176,2048]{2,1,0:T(8,128)(2,1)}), bf16[1,1408,2048]{2,1,0:T(8,128)(2,1)}) %all-gather.9.cloned.1.call-update) | async-done | bytes 5767184 | tf_op jit(solution)/shard_map/all_gather | solution.py:117
  159.6 7.4 %fusion.3 = bf16[128,2048]{1,0:T(8,128)(2,1)S(1)} fusion(bf16[1,1408,2048]{2,1,0:T(8,128)(2,1)} %all-gather.9.cloned.1.call-done, bf16[128,2048]{1,0:T(8,128)(2,1)S(1)} %reshape.158, bf16[1408,2048]{1,0:T(8,128)(2,1)} %all-gather.7.cloned.1.call-done, f32[128,1408]{1,0:T(8,128)S(1)} %fusion.17), kind=kOutput, calls=%fused_computation.5 | convolution fusion | flops 1477738496 | bytes 13303808 | tf_op jit(solution)/shard_map/dot_general | solution.py:177
  167.0 1.1 reshape.159
  168.1 15.4 %all-to-all-start.3 = ((bf16[64,2,2048]{2,1,0:T(2,128)(2,1)}), bf16[64,2,2048]{2,1,0:T(2,128)(2,1)S(1)}, u32[]{:S(2)}, u32[]{:S(2)}) async-start(bf16[64,2,2048]{2,1,0:T(2,128)(2,1)} %reshape.159), calls=%async_computation.3 | async-start | bytes 1048576 | tf_op jit(solution)/shard_map/all_to_all | solution.py:178
  183.7 0.7 select_reduce_fusion.2.gate_ref
  184.4 30.3 %all-to-all-done.3 = bf16[64,2,2048]{2,1,0:T(2,128)(2,1)S(1)} async-done(((bf16[64,2,2048]{2,1,0:T(2,128)(2,1)}), bf16[64,2,2048]{2,1,0:T(2,128)(2,1)S(1)}, u32[]{:S(2)}, u32[]{:S(2)}) %all-to-all-start.3) | async-done | bytes 524320 | tf_op jit(solution)/shard_map/all_to_all | solution.py:178
  214.6 1.0 reshape.160.rows_ref
  215.6 2.0 combine.1
  217.6 10.9 %all_to_all.26 = bf16[8,16,256]{2,1,0:T(8,128)(2,1)S(1)} all-to-all(bf16[8,16,256]{2,1,0:T(8,128)(2,1)} %combine.1), channel_id=1, replica_groups=mesh['section'=2,'dp'=64,'mp'=4] {'section','mp'}, dimensions={0} | all-to-all | bytes 131072 | tf_op jit(solution)/shard_map/all_to_all | solution.py:186
  228.5 0.6 copy.40
  (43 shorter events, 2.9 us)
Async XLA Ops:
  6.5 80.8 %copy-start = (bf16[128,2048]{1,0:T(8,128)(2,1)S(1)}, bf16[128,2048]{1,0:T(8,128)(2,1)}, u32[]{:S(2)}) copy-start(bf16[128,2048]{1,0:T(8,128)(2,1)} %param.16) | copy-start | bytes 1572868
  6.5 26.4 %copy-start.6 = (s32[1,1,4]{2,1,0:T(1,128)S(1)}, s32[1,1,4]{2,1,0:T(1,128)}, u32[]{:S(2)}) copy-start(s32[1,1,4]{2,1,0:T(1,128)} %param.23) | copy-start | bytes 52
  6.5 28.9 %copy-start.5 = (s32[1,1,128]{2,1,0:T(1,128)S(1)}, s32[1,1,128]{2,1,0:T(1,128)}, u32[]{:S(2)}) copy-start(s32[1,1,128]{2,1,0:T(1,128)} %param.22) | copy-start | bytes 1540
  6.5 29.7 %copy-start.3 = (s32[128,4]{0,1:T(4,128)S(1)}, s32[128,4]{0,1:T(4,128)}, u32[]{:S(2)}) copy-start(s32[128,4]{0,1:T(4,128)} %param.26) | copy-start | bytes 6148
  6.5 135.0 %all-gather.5.cloned.1.call-start = ((), (), s32[]{:S(2)}) async-start(), calls=%async_computation.5 | async-start | bytes 6488064 | tf_op jit(solution)/shard_map/all_gather | solution.py:115
  7.3 139.1 %all-gather.7.cloned.1.call-start = ((), (), s32[]{:S(2)}) async-start(), calls=%async_computation.6 | async-start | bytes 6488064 | tf_op jit(solution)/shard_map/all_gather | solution.py:116
  8.0 151.5 %all-gather.9.cloned.1.call-start = ((), (), s32[]{:S(2)}) async-start(), calls=%async_computation.7 | async-start | bytes 6488064 | tf_op jit(solution)/shard_map/all_gather | solution.py:117
  13.7 60.0 %all-to-all-start = ((bf16[64,3,8,256]{3,2,1,0:T(8,128)(2,1)}), bf16[64,3,8,256]{3,2,1,0:T(8,128)(2,1)S(1)}, u32[]{:S(2)}, u32[]{:S(2)}) async-start(bf16[64,3,8,256]{3,2,1,0:T(8,128)(2,1)} %bitcast.2), calls=%async_computation | async-start | bytes 1572864 | tf_op jit(solution)/shard_map/all_to_all | solution.py:113
  73.6 0.9 copy-start.1
  77.8 21.5 %all-to-all-start.1 = ((bf16[8,16,2048]{2,1,0:T(8,128)(2,1)}), bf16[8,16,2048]{2,1,0:T(8,128)(2,1)S(1)}, u32[]{:S(2)}, u32[]{:S(2)}) async-start(bf16[8,16,2048]{2,1,0:T(8,128)(2,1)} %bitcast.35), calls=%async_computation.1 | async-start | bytes 1048576 | tf_op jit(solution)/shard_map/all_to_all | solution.py:159
  99.3 0.8 copy-start.2
  146.3 37.3 %copy-start.4 = (f32[128,4]{0,1:T(4,128)S(1)}, f32[128,4]{0,1:T(4,128)}, u32[]{:S(2)}) copy-start(f32[128,4]{0,1:T(4,128)} %param.27) | copy-start | bytes 6148
  168.1 46.5 %all-to-all-start.3 = ((bf16[64,2,2048]{2,1,0:T(2,128)(2,1)}), bf16[64,2,2048]{2,1,0:T(2,128)(2,1)S(1)}, u32[]{:S(2)}, u32[]{:S(2)}) async-start(bf16[64,2,2048]{2,1,0:T(2,128)(2,1)} %reshape.159), calls=%async_computation.3 | async-start | bytes 1048576 | tf_op jit(solution)/shard_map/all_to_all | solution.py:178
Sparse Core Ops, SparseCore 0:
  9.5 52.0 all-gather.4
  63.8 52.0 all-gather.6
  118.1 41.4 all-gather.8

commit v2 on v1

--- a/solution.py
+++ b/solution.py
@@ -8,11 +8,14 @@
 from jax.sharding import PartitionSpec as P
 
 HEAD_DIM = 128
+LANES = 128
 TOPK = 4
 PREF = 64
 BLK = 8
 OWN_CAP = 3
 CAPQ = 2
+PIECES = 4
+CHUNKS = (2, 2, 2, 1, 1)
 SPLIT = ("section", "mp")
 
 
@@ -48,6 +51,80 @@
     ).astype(out_ref.dtype)
 
 
+def in_vmem(x):
+    return pltpu.with_memory_space_constraint(x, pltpu.VMEM)
+
+
+def in_hbm(x):
+    return pltpu.with_memory_space_constraint(x, pltpu.HBM)
+
+
+def select_kernel(
+    owners_ref,
+    slots_ref,
+    cache_ref,
+    gate_hbm,
+    up_hbm,
+    down_hbm,
+    out_ref,
+    pack_hbm,
+    cache_wide,
+    out_wide,
+    pack_buf,
+    sems,
+):
+    unit = gate_hbm.shape[0]
+    parts = [pl.ds(i * unit, unit) for i in range(3)]
+    loads = [
+        pltpu.make_async_copy(source, pack_buf.at[part], sems.at[0, i])
+        for i, (source, part) in enumerate(zip((gate_hbm, up_hbm, down_hbm), parts))
+    ]
+    stores = [
+        pltpu.make_async_copy(pack_buf.at[part], pack_hbm.at[part], sems.at[1, i])
+        for i, part in enumerate(parts)
+    ]
+    for load in loads:
+        load.start()
+    halves = cache_wide.shape[0]
+    for h in range(halves):
+        cache_wide[h] = cache_ref[:, h * LANES : (h + 1) * LANES].astype(jnp.float32)
+    owned = owners_ref[:, 0, :] == lax.axis_index("dp")
+    named = slots_ref[:, 0, :]
+    groups, entries = owned.shape
+    earlier = lax.broadcasted_iota(jnp.int32, (entries, entries), 0) < lax.broadcasted_iota(
+        jnp.int32, (entries, entries), 1
+    )
+    rank = jnp.dot(
+        jnp.where(owned, 1.0, 0.0).astype(jnp.bfloat16),
+        jnp.where(earlier, 1.0, 0.0).astype(jnp.bfloat16),
+        preferred_element_type=jnp.float32,
+    )
+    held = cache_ref.shape[0] // BLK
+    index = lax.broadcasted_iota(jnp.int32, (groups, held), 1)
+    picks = []
+    for r in range(OWN_CAP):
+        slot = jnp.sum(jnp.where(owned & (rank == r), named, 0), axis=1, keepdims=True)
+        picks.append(jnp.where(slot == index, 1.0, 0.0).astype(jnp.bfloat16))
+    picks = jnp.concatenate(picks, axis=0)
+    for load, store in zip(loads, stores):
+        load.wait()
+        store.start()
+    for b in range(BLK):
+        part = jnp.concatenate(
+            [cache_wide[h, pl.ds(b, held, stride=BLK), :] for h in range(halves)], axis=1
+        )
+        chosen = jnp.dot(picks, part.astype(jnp.bfloat16), preferred_element_type=jnp.float32)
+        for r in range(OWN_CAP):
+            for h in range(halves):
+                out_wide[h, pl.ds(r * BLK + b, groups, stride=OWN_CAP * BLK), :] = chosen[
+                    r * groups : (r + 1) * groups, h * LANES : (h + 1) * LANES
+                ]
+    for h in range(halves):
+        out_ref[:, h * LANES : (h + 1) * LANES] = out_wide[h].astype(jnp.bfloat16)
+    for store in stores:
+        store.wait()
+
+
 def norm_kernel(parts_ref, residual_ref, gain_ref, pick_ref, mixed_ref, out_ref):
     mixed = residual_ref[...].astype(jnp.float32)
     projected = parts_ref[0].astype(jnp.float32)
@@ -57,9 +134,60 @@
     mixed_ref[...] = mixed
     square = jnp.mean(mixed * mixed, axis=1, keepdims=True)
     normed = (mixed * lax.rsqrt(square + 1e-06) * gain_ref[...]).astype(jnp.bfloat16)
-    out_ref[...] = jnp.dot(pick_ref[...], normed, preferred_element_type=jnp.float32).astype(
+    out_ref[...] = jnp.dot(
+        pick_ref[...], stack_pieces(normed), preferred_element_type=jnp.float32
+    ).astype(jnp.bfloat16)
+
+
+def stack_pieces(x):
+    cols = x.shape[1] // PIECES
+    return jnp.concatenate([x[:, i * cols : (i + 1) * cols] for i in range(PIECES)], axis=0)
+
+
+def join_pieces(x):
+    rows = x.shape[0] // PIECES
+    return jnp.concatenate([x[i * rows : (i + 1) * rows] for i in range(PIECES)], axis=1)
+
+
+def ffn_kernel(x_ref, weight_hbm, out_ref, weight_ref, sems):
+    shards, _, unit, width = weight_ref.shape
+    ends = [sum(CHUNKS[: i + 1]) for i in range(len(CHUNKS))]
+    spans = [(end - size, size) for end, size in zip(ends, CHUNKS)]
+    assert ends[-1] == shards
+    copies = [
+        pltpu.make_async_copy(
+            weight_hbm.at[pl.ds(first, size)], weight_ref.at[pl.ds(first, size)], sems.at[i]
+        )
+        for i, (first, size) in enumerate(spans)
+    ]
+    ahead = 3
+    for copy in copies[:ahead]:
+        copy.start()
+    total = x_ref.shape[0]
+    rows = total // PIECES
+    near = lax.broadcasted_iota(jnp.int32, (total, total), 0)
+    far = lax.broadcasted_iota(jnp.int32, (total, total), 1)
+    to_rows = jnp.where(far == (near % rows) * PIECES + near // rows, 1.0, 0.0).astype(jnp.bfloat16)
+    to_pieces = jnp.where(near == (far % rows) * PIECES + far // rows, 1.0, 0.0).astype(
         jnp.bfloat16
     )
+    x = join_pieces(
+        jnp.dot(to_rows, x_ref[...], preferred_element_type=jnp.float32).astype(jnp.bfloat16)
+    )
+    result = jnp.zeros((rows, width), jnp.float32)
+    for i, (first, size) in enumerate(spans):
+        copies[i].wait()
+        if i + ahead < len(copies):
+            copies[i + ahead].start()
+        gate, up, down = (
+            weight_ref[first : first + size, j].reshape(size * unit, width) for j in range(3)
+        )
+        gate = nt_dot(x, gate)
+        hidden = (gate / (1.0 + jnp.exp(-gate)) * nt_dot(x, up)).astype(jnp.bfloat16)
+        result = result + jnp.dot(hidden, down, preferred_element_type=jnp.float32)
+    out_ref[...] = jnp.dot(
+        to_pieces, stack_pieces(result.astype(jnp.bfloat16)), preferred_element_type=jnp.float32
+    ).astype(jnp.bfloat16)
 
 
 def combine_kernel(rows_ref, gate_ref, mixed_ref, out_ref):
@@ -69,7 +197,7 @@
     rows = rows_ref[...]
     total = jnp.dot(high, rows, preferred_element_type=jnp.float32)
     total = total + jnp.dot(low, rows, preferred_element_type=jnp.float32)
-    total = (total + mixed_ref[...]).astype(jnp.bfloat16)
+    total = (join_pieces(total) + mixed_ref[...]).astype(jnp.bfloat16)
     cols = out_ref.shape[2]
     for i in range(out_ref.shape[0]):
         out_ref[i] = total[:, i * cols : (i + 1) * cols]
@@ -101,20 +229,45 @@
     cols = width // shards
     slots = groups * CAPQ
 
+    vmem = pl.BlockSpec(memory_space=pltpu.VMEM)
+    hbm = pl.BlockSpec(memory_space=pltpu.HBM)
     table = owners[:, 0, :, 0]
-    owned = table == group
-    order = jnp.cumsum(owned.astype(jnp.int32), axis=1) - 1
-    wanted = owned[:, None, :] & (
-        order[:, None, :] == jnp.arange(OWN_CAP, dtype=jnp.int32)[None, :, None]
-    )
-    pick = jnp.sum(jnp.where(wanted, slot_ids[:, 0, :][:, None, :], 0), axis=2)
-    chosen = kv_cache.at[pick.reshape(-1)].get(mode="promise_in_bounds")
-    chosen = chosen.reshape(groups, OWN_CAP, BLK, kv_cache.shape[2])
-    arrived = lax.all_to_all(chosen, "dp", split_axis=0, concat_axis=0, tiled=True)
-
-    full_gate = lax.all_gather(w_gate[0].T, SPLIT, axis=0, tiled=True)
-    full_up = lax.all_gather(w_up[0].T, SPLIT, axis=0, tiled=True)
-    full_down = lax.all_gather(w_down[0], SPLIT, axis=0, tiled=True)
+    unit = w_down.shape[1]
+    cache_cols = kv_cache.shape[2]
+    cache_rows = kv_cache.shape[0] * BLK
+    sent_rows = groups * OWN_CAP * BLK
+    chosen, packed = pl.pallas_call(
+        select_kernel,
+        in_specs=[vmem, vmem, vmem, hbm, hbm, hbm],
+        out_specs=(vmem, hbm),
+        out_shape=(
+            pltpu.VMEM((sent_rows, cache_cols), jnp.bfloat16),
+            pltpu.HBM((3 * unit, width), jnp.bfloat16),
+        ),
+        scratch_shapes=[
+            pltpu.VMEM((cache_cols // LANES, cache_rows, LANES), jnp.float32),
+            pltpu.VMEM((cache_cols // LANES, sent_rows, LANES), jnp.float32),
+            pltpu.VMEM((3 * unit, width), jnp.bfloat16),
+            pltpu.SemaphoreType.DMA((2, 3)),
+        ],
+        compiler_params=pltpu.CompilerParams(vmem_limit_bytes=12 << 20),
+        name="select",
+    )(
+        in_hbm(owners[:, :, :, 0]),
+        in_hbm(slot_ids),
+        in_hbm(kv_cache.reshape(cache_rows, cache_cols)),
+        in_hbm(w_gate[0].T),
+        in_hbm(w_up[0].T),
+        in_hbm(w_down[0]),
+    )
+    arrived = lax.all_to_all(
+        chosen.reshape(groups, OWN_CAP, BLK, cache_cols),
+        "dp",
+        split_axis=0,
+        concat_axis=0,
+        tiled=True,
+    )
+    full = lax.all_gather(packed, SPLIT, axis=0, tiled=True)
 
     mine = lax.dynamic_index_in_dim(table, group, 0, keepdims=False)
     index = jnp.arange(PREF, dtype=jnp.int32)
@@ -137,52 +290,81 @@
     same = (flat[None, :] == flat[:, None]) & (pair[None, :] < pair[:, None])
     slot = (flat * CAPQ + jnp.sum(same.astype(jnp.int32), axis=1)).reshape(block, TOPK)
     slot_index = jnp.arange(slots, dtype=jnp.int32)
-    hit = slot[:, :, None] == slot_index[None, None, :]
-    gate_matrix = jnp.sum(jnp.where(hit, gates[:, :, None], 0.0), axis=1)
-    pick_matrix = jnp.any(slot.T[None, :, :] == slot_index[:, None, None], axis=1).astype(
-        jnp.bfloat16
-    )
+    line = jnp.arange(slots * PIECES, dtype=jnp.int32)
+    piece = jnp.arange(PIECES, dtype=jnp.int32)
+    hit = slot[:, :, None] == line[None, None, :] // PIECES
+    mine_of_piece = (line[None, :] % PIECES == piece[:, None])[:, None, :]
+    gate_matrix = jnp.where(
+        mine_of_piece, jnp.sum(jnp.where(hit, gates[:, :, None], 0.0), axis=1)[None], 0.0
+    ).reshape(PIECES * block, -1)
+    pick_matrix = (
+        (mine_of_piece & jnp.any(hit, axis=1)[None]).reshape(PIECES * block, -1).T
+    ).astype(jnp.bfloat16)
     my_residual = lax.dynamic_slice_in_dim(residual, first, block, 0)
 
+    lines = slots * PIECES
+    piece_cols = width // PIECES
     projected = pl.pallas_call(
         attend_kernel,
-        out_shape=jax.ShapeDtypeStruct((rows, width), jnp.bfloat16),
+        in_specs=[vmem] * 6,
+        out_specs=vmem,
+        out_shape=pltpu.VMEM((rows, width), jnp.bfloat16),
         name="attend",
     )(
-        qkv,
-        arrived.reshape(-1, kv_cache.shape[2]),
-        key_seg,
-        segments[None, :],
-        segments[:, None],
-        out_weight,
+        in_hbm(qkv),
+        in_vmem(arrived.reshape(-1, kv_cache.shape[2])),
+        in_vmem(key_seg),
+        in_hbm(segments[None, :]),
+        in_vmem(segments[:, None]),
+        in_hbm(out_weight),
     )
     parts = lax.all_to_all(
         projected.reshape(shards, block, width), SPLIT, split_axis=0, concat_axis=0, tiled=True
     )
     mixed, outgoing = pl.pallas_call(
         norm_kernel,
+        in_specs=[vmem] * 4,
+        out_specs=(vmem, vmem),
         out_shape=(
-            jax.ShapeDtypeStruct((block, width), jnp.float32),
-            jax.ShapeDtypeStruct((slots, width), jnp.bfloat16),
+            pltpu.VMEM((block, width), jnp.float32),
+            pltpu.VMEM((lines, piece_cols), jnp.bfloat16),
         ),
         name="norm",
-    )(parts, my_residual, moe_gain[None, :], pick_matrix)
+    )(in_vmem(parts), in_vmem(my_residual), in_hbm(moe_gain[None, :]), in_vmem(pick_matrix))
     incoming = lax.all_to_all(
-        outgoing.reshape(groups, CAPQ, width), "dp", split_axis=0, concat_axis=0, tiled=True
-    ).reshape(slots, width)
-
-    hidden = (jax.nn.silu(nt_dot(incoming, full_gate)) * nt_dot(incoming, full_up)).astype(
-        jnp.bfloat16
-    )
-    produced = jnp.dot(hidden, full_down, preferred_element_type=jnp.float32).astype(jnp.bfloat16)
+        outgoing.reshape(groups, CAPQ * PIECES, piece_cols),
+        "dp",
+        split_axis=0,
+        concat_axis=0,
+        tiled=True,
+    ).reshape(lines, piece_cols)
+
+    produced = pl.pallas_call(
+        ffn_kernel,
+        in_specs=[vmem, hbm],
+        out_specs=vmem,
+        out_shape=pltpu.VMEM((lines, piece_cols), jnp.bfloat16),
+        scratch_shapes=[
+            pltpu.VMEM((shards, 3, unit, width), jnp.bfloat16),
+            pltpu.SemaphoreType.DMA((len(CHUNKS),)),
+        ],
+        compiler_params=pltpu.CompilerParams(vmem_limit_bytes=40 << 20),
+        name="ffn",
+    )(in_vmem(incoming), in_hbm(full.reshape(shards, 3, unit, width)))
     returned = lax.all_to_all(
-        produced.reshape(groups, CAPQ, width), "dp", split_axis=0, concat_axis=0, tiled=True
-    ).reshape(slots, width)
+        produced.reshape(groups, CAPQ * PIECES, piece_cols),
+        "dp",
+        split_axis=0,
+        concat_axis=0,
+        tiled=True,
+    ).reshape(lines, piece_cols)
     finished = pl.pallas_call(
         combine_kernel,
-        out_shape=jax.ShapeDtypeStruct((shards, block, cols), jnp.bfloat16),
+        in_specs=[vmem] * 3,
+        out_specs=vmem,
+        out_shape=pltpu.VMEM((shards, block, cols), jnp.bfloat16),
         name="combine",
-    )(returned, gate_matrix, mixed)
+    )(in_vmem(returned), in_vmem(gate_matrix), in_vmem(mixed))
     result = lax.all_to_all(finished, SPLIT, split_axis=0, concat_axis=0, tiled=True)
     return result.reshape(rows, cols)
 

time: 236 us -> 201 us (0.85)
  waiting for transfers between devices: 93.8 us -> 77.7 us
  matrix products: 12.1 us -> 0 us
  Pallas kernels: 7.56 us -> 18.3 us
  local copies, waits for them, and re-layouts: 12.9 us -> 3.37 us
  starting transfers between devices: 43.4 us -> 34.7 us
    all_gather x3 -> x1, waiting for transfers between devices: 13.3 us -> 0.01 us  [local(): full = lax.all_gather(packed, SPLIT, axis=0, tiled=True)]
    dot_general x2 -> x0, matrix products: 12.1 us -> none  [the longest x1 7.43 us: local(): jnp.dot(hidden, full_down, preferred_element_type=jnp.float32)]
    pallas_call x3 -> x5, Pallas kernels: 7.56 us -> 18.3 us  [the longest x1 9.39 us: local(): pl.pallas_call(ffn_kernel, in_specs=[vmem, hbm], out_specs=vmem, out_shap...]
    all_to_all x2, starting transfers between devices: 34.6 us -> 26 us  [the longest x1 19.3 us: local(): lax.all_to_all(chosen.reshape(groups, OWN_CAP, BLK, cache_cols), 'dp', sp...]
    reshape x5 -> x0, local copies, waits for them, and re-layouts: 3.84 us -> none  [the longest x1 1.38 us: local(): outgoing.reshape(groups, CAPQ, width)]
    all_to_all x1, blocking collectives: 10.9 us -> 13.9 us  [local(): lax.all_to_all(finished, SPLIT, split_axis=0, concat_axis=0, tiled=True)]
    gather x1 -> x0, local copies, waits for them, and re-layouts: 2.67 us -> none  [local(): chosen = kv_cache.at[pick.reshape(-1)].get(mode='promise_in_bounds')]
  transfers between devices with their start and end apart: 6 -> 4, of which waited for: 4 -> 3; matrix products, arithmetic and copies ran while one was open for 7% -> 3% of each run, Pallas kernels for 2% -> 2%
where the time goes in v2:
time: 201 us
  waiting for transfers between devices  77.7 us (39%)
  blocking collectives  50.7 us (25%)
  starting transfers between devices  34.7 us (17%)
  Pallas kernels  18.3 us (9%)
  between operations  13.6 us (7%)
  local copies, waits for them, and re-layouts  3.37 us (2%)
  other arithmetic  2.31 us (1%)
    all_to_all x1, blocking collectives, local(): lax.all_to_all(outgoing.reshape(groups, CAPQ * PIECES, piece_cols), 'dp',...  36.8 us
    all_to_all x1, waiting for transfers between devices, local(): lax.all_to_all(chosen.reshape(groups, OWN_CAP, BLK, cache_cols), 'dp', sp...  36 us
    all_to_all x1, waiting for transfers between devices, local(): lax.all_to_all(produced.reshape(groups, CAPQ * PIECES, piece_cols), 'dp',...  29.1 us
    all_to_all x1, starting transfers between devices, local(): lax.all_to_all(chosen.reshape(groups, OWN_CAP, BLK, cache_cols), 'dp', sp...  19.3 us
    all_to_all x1, blocking collectives, local(): lax.all_to_all(finished, SPLIT, split_axis=0, concat_axis=0, tiled=True)  13.9 us
    all_to_all x1, waiting for transfers between devices, local(): lax.all_to_all(projected.reshape(shards, block, width), SPLIT, split_axis...  12.6 us
    pallas_call x1, Pallas kernels, local(): pl.pallas_call(ffn_kernel, in_specs=[vmem, hbm], out_specs=vmem, out_shap...  9.39 us
    all_to_all x1, starting transfers between devices, local(): lax.all_to_all(projected.reshape(shards, block, width), SPLIT, split_axis...  8.72 us
  transfers between devices with their start and end apart: 4, of which 3 were waited for; matrix products, arithmetic and copies ran while one was open for 3% of the time, Pallas kernels for 2%

profile of v2, /device:TPU:1, one launch (start us, length us, event | category | flops | bytes accessed | tf_op | source)
XLA Modules:
  0.0 200.6 jit_solution(1773136073610453044)
XLA Ops:
  6.5 4.5 %select.23 = (bf16[1536,256]{1,0:T(8,128)(2,1)}, bf16[528,2048]{1,0:T(8,128)(2,1)}) custom-call(s32[64,1,64]{2,1,0:T(1,128)} %bitcast.43, s32[64,1,64]{2,1,0:T(1,128)} %slots_ref.1, bf16[512,256]{1,0:T(8,128)(2,1)} %bitcast.40, bf16[176,2048]{1,0:T(8,128)(2,1)} %bitcast.37, bf16[176,2048]{1,0:T(8,128)(2,1)} %bitcast.38, bf16[176,2048]{1,0:T(8,128)(2,1)} %bitcast.39), custom_call_target="tpu_custom_call" | custom-call | tf_op jit(solution)/shard_map/select/pallas_call | solution.py:239
  11.0 0.0 all-gather.2.cloned.1.call-update
  11.1 19.3 %all-to-all-start = ((bf16[64,3,8,256]{3,2,1,0:T(8,128)(2,1)}), bf16[64,3,8,256]{3,2,1,0:T(8,128)(2,1)S(1)}, u32[]{:S(2)}, u32[]{:S(2)}) async-start(bf16[64,3,8,256]{3,2,1,0:T(8,128)(2,1)} %bitcast.7), calls=%async_computation | async-start | bytes 1572864 | tf_op jit(solution)/shard_map/all_to_all | solution.py:263
  30.4 0.8 constant_dynamic-slice_fusion
  31.1 0.1 copy.27
  31.2 0.1 eq.88
  31.3 0.2 convert_reduce_fusion
  31.5 0.1 reduce_sum.51
  31.6 0.1 copy.25
  31.7 0.8 reduce-window.8
  32.5 0.7 fusion.11
  33.2 0.1 convert_reduce_fusion.2
  33.2 0.2 convert_reduce_fusion.1
  33.4 0.7 multiply_add_fusion.1
  34.1 0.1 select_reduce_fusion
  34.3 0.8 copy.23.seg_col_ref
  35.0 36.0 %all-to-all-done = bf16[64,3,8,256]{3,2,1,0:T(8,128)(2,1)S(1)} async-done(((bf16[64,3,8,256]{3,2,1,0:T(8,128)(2,1)}), bf16[64,3,8,256]{3,2,1,0:T(8,128)(2,1)S(1)}, u32[]{:S(2)}, u32[]{:S(2)}) %all-to-all-start) | async-done | bytes 786464 | tf_op jit(solution)/shard_map/all_to_all | solution.py:263
  71.0 3.0 %attend.1 = bf16[128,2048]{1,0:T(8,128)(2,1)} custom-call(bf16[128,384]{1,0:T(8,128)(2,1)} %qkv_ref.1, bf16[1536,256]{1,0:T(8,128)(2,1)S(1)} %bitcast.30, s32[1,1536]{1,0:T(1,128)S(1)} %sub.20.key_seg_ref, s32[1,128]{1,0:T(1,128)} %bitcast.46, s32[128,1]{1,0:T(8,128)S(1)} %copy.23.seg_col_ref, bf16[128,2048]{1,0:T(8,128)(2,1)} %weight_ref.1), custom_call_target="tpu_custom_call" | custom-call | tf_op jit(solution)/shard_map/attend/pallas_call | solution.py:307
  74.0 8.7 %all-to-all-start.1 = ((bf16[8,16,2048]{2,1,0:T(8,128)(2,1)}), bf16[8,16,2048]{2,1,0:T(8,128)(2,1)S(1)}, u32[]{:S(2)}, u32[]{:S(2)}) async-start(bf16[8,16,2048]{2,1,0:T(8,128)(2,1)} %bitcast.14), calls=%async_computation.1 | async-start | bytes 1048576 | tf_op jit(solution)/shard_map/all_to_all | solution.py:321
  82.8 0.1 compare_reduce_fusion
  82.9 0.1 copy.26
  83.0 12.6 %all-to-all-done.1.parts_ref = bf16[8,16,2048]{2,1,0:T(8,128)(2,1)S(1)} async-done(((bf16[8,16,2048]{2,1,0:T(8,128)(2,1)}), bf16[8,16,2048]{2,1,0:T(8,128)(2,1)S(1)}, u32[]{:S(2)}, u32[]{:S(2)}) %all-to-all-start.1) | async-done | bytes 524320 | tf_op jit(solution)/shard_map/all_to_all | solution.py:321
  95.6 1.1 norm.1
  96.7 36.8 %all_to_all.25 = bf16[64,8,512]{2,1,0:T(8,128)(2,1)S(1)} all-to-all(bf16[64,8,512]{2,1,0:T(8,128)(2,1)S(1)} %bitcast.33), channel_id=1, replica_groups=mesh['section'=2,'dp'=64,'mp'=4] {'dp'}, dimensions={0} | all-to-all | bytes 1048576 | tf_op jit(solution)/shard_map/all_to_all | solution.py:334
  133.5 9.4 %ffn.1 = bf16[512,512]{1,0:T(8,128)(2,1)} custom-call(bf16[512,512]{1,0:T(8,128)(2,1)S(1)} %bitcast.31, bf16[8,3,176,2048]{3,2,1,0:T(8,128)(2,1)} %bitcast.36), custom_call_target="tpu_custom_call" | custom-call | tf_op jit(solution)/shard_map/ffn/pallas_call | solution.py:342
  142.9 6.7 %all-to-all-start.3 = ((bf16[64,8,512]{2,1,0:T(8,128)(2,1)}), bf16[64,8,512]{2,1,0:T(8,128)(2,1)S(1)}, u32[]{:S(2)}, u32[]{:S(2)}) async-start(bf16[64,8,512]{2,1,0:T(8,128)(2,1)} %bitcast.21), calls=%async_computation.3 | async-start | bytes 1048576 | tf_op jit(solution)/shard_map/all_to_all | solution.py:354
  149.6 0.1 constant_dynamic-slice_fusion.2
  149.7 0.1 fusion
  149.8 29.1 %all-to-all-done.3 = bf16[64,8,512]{2,1,0:T(8,128)(2,1)S(1)} async-done(((bf16[64,8,512]{2,1,0:T(8,128)(2,1)}), bf16[64,8,512]{2,1,0:T(8,128)(2,1)S(1)}, u32[]{:S(2)}, u32[]{:S(2)}) %all-to-all-start.3) | async-done | bytes 524320 | tf_op jit(solution)/shard_map/all_to_all | solution.py:354
  178.9 0.3 combine.1
  179.2 13.9 %all_to_all.26 = bf16[8,16,256]{2,1,0:T(8,128)(2,1)S(1)} all-to-all(bf16[8,16,256]{2,1,0:T(8,128)(2,1)S(1)} %combine.1), channel_id=1, replica_groups=mesh['section'=2,'dp'=64,'mp'=4] {'section','mp'}, dimensions={0} | all-to-all | bytes 131072 | tf_op jit(solution)/shard_map/all_to_all | solution.py:368
  193.1 0.6 copy.29
  (17 shorter events, 0.1 us)
Async XLA Ops:
  6.5 76.5 %copy-start = (bf16[128,2048]{1,0:T(8,128)(2,1)S(1)}, bf16[128,2048]{1,0:T(8,128)(2,1)}, u32[]{:S(2)}) copy-start(bf16[128,2048]{1,0:T(8,128)(2,1)} %param.16) | copy-start | bytes 1572868
  6.5 143.1 %copy-start.1 = (f32[128,4]{0,1:T(4,128)S(1)}, f32[128,4]{0,1:T(4,128)}, u32[]{:S(2)}) copy-start(f32[128,4]{0,1:T(4,128)} %param.27) | copy-start | bytes 6148
  6.5 127.0 %all-gather.2.cloned.1.call-start = ((), (), s32[]{:S(2)}) async-start(), calls=%async_computation.5 | async-start | bytes 19464192 | tf_op jit(solution)/shard_map/all_gather | solution.py:270
  11.1 60.0 %all-to-all-start = ((bf16[64,3,8,256]{3,2,1,0:T(8,128)(2,1)}), bf16[64,3,8,256]{3,2,1,0:T(8,128)(2,1)S(1)}, u32[]{:S(2)}, u32[]{:S(2)}) async-start(bf16[64,3,8,256]{3,2,1,0:T(8,128)(2,1)} %bitcast.7), calls=%async_computation | async-start | bytes 1572864 | tf_op jit(solution)/shard_map/all_to_all | solution.py:263
  74.0 21.6 %all-to-all-start.1 = ((bf16[8,16,2048]{2,1,0:T(8,128)(2,1)}), bf16[8,16,2048]{2,1,0:T(8,128)(2,1)S(1)}, u32[]{:S(2)}, u32[]{:S(2)}) async-start(bf16[8,16,2048]{2,1,0:T(8,128)(2,1)} %bitcast.14), calls=%async_computation.1 | async-start | bytes 1048576 | tf_op jit(solution)/shard_map/all_to_all | solution.py:321
  142.9 36.0 %all-to-all-start.3 = ((bf16[64,8,512]{2,1,0:T(8,128)(2,1)}), bf16[64,8,512]{2,1,0:T(8,128)(2,1)S(1)}, u32[]{:S(2)}, u32[]{:S(2)}) async-start(bf16[64,8,512]{2,1,0:T(8,128)(2,1)} %bitcast.21), calls=%async_computation.3 | async-start | bytes 1048576 | tf_op jit(solution)/shard_map/all_to_all | solution.py:354
Sparse Core Ops, SparseCore 0:
  11.2 106.1 all-gather.1

commit v3 on v2

--- a/solution.py
+++ b/solution.py
@@ -23,7 +23,9 @@
     return lax.dot_general(a, b, (((1,), (1,)), ((), ())), preferred_element_type=jnp.float32)
 
 
-def attend_kernel(qkv_ref, prefix_ref, key_seg_ref, seg_row_ref, seg_col_ref, weight_ref, out_ref):
+def attend_kernel(
+    qkv_ref, prefix_ref, key_seg_ref, seg_row_ref, seg_col_ref, weight_ref, keep_ref, send_ref, rows_ref
+):
     rows = qkv_ref.shape[0]
     query = qkv_ref[:, :HEAD_DIM]
     scale = 1.0 / math.sqrt(HEAD_DIM)
@@ -46,9 +48,18 @@
     attended = jnp.dot(
         old, prefix_ref[:, HEAD_DIM:], preferred_element_type=jnp.float32
     ) + jnp.dot(new, qkv_ref[:, 2 * HEAD_DIM :], preferred_element_type=jnp.float32)
-    out_ref[...] = jnp.dot(
-        attended.astype(jnp.bfloat16), weight_ref[...], preferred_element_type=jnp.float32
-    ).astype(out_ref.dtype)
+    rows_ref[...] = attended.astype(jnp.bfloat16)
+    half = keep_ref.shape[0]
+    core = lax.axis_index("section")
+    for ref, side in ((keep_ref, core), (send_ref, 1 - core)):
+        part = rows_ref[pl.ds(pl.multiple_of(side * half, half), half), :]
+        ref[...] = jnp.dot(
+            part, weight_ref[...], preferred_element_type=jnp.float32
+        ).astype(ref.dtype)
+
+
+def add_kernel(a_ref, b_ref, out_ref):
+    out_ref[...] = (a_ref[...] + b_ref[...].astype(jnp.float32)).astype(out_ref.dtype)
 
 
 def in_vmem(x):
@@ -59,37 +70,59 @@
     return pltpu.with_memory_space_constraint(x, pltpu.HBM)
 
 
+def fetch_kernel(*refs):
+    count = len(refs) // 2
+    sems = refs[-1]
+    copies = [
+        pltpu.make_async_copy(refs[i], refs[count + i], sems.at[i]) for i in range(count)
+    ]
+    for copy in copies:
+        copy.start()
+    for copy in copies:
+        copy.wait()
+
+
 def select_kernel(
+    owners_hbm,
+    slots_hbm,
+    cache_hbm,
+    gate_hbm,
+    up_hbm,
+    down_hbm,
+    out_hbm,
+    pack_hbm,
     owners_ref,
     slots_ref,
     cache_ref,
-    gate_hbm,
-    up_hbm,
-    down_hbm,
-    out_ref,
-    pack_hbm,
     cache_wide,
     out_wide,
+    out_ref,
     pack_buf,
-    sems,
+    table_sems,
+    load_sems,
+    store_sems,
+    out_sems,
 ):
     unit = gate_hbm.shape[0]
+    tables = [
+        pltpu.make_async_copy(source, target, table_sems.at[i])
+        for i, (source, target) in enumerate(
+            ((owners_hbm, owners_ref), (slots_hbm, slots_ref), (cache_hbm, cache_ref))
+        )
+    ]
     parts = [pl.ds(i * unit, unit) for i in range(3)]
     loads = [
-        pltpu.make_async_copy(source, pack_buf.at[part], sems.at[0, i])
+        pltpu.make_async_copy(source, pack_buf.at[part], load_sems.at[i])
         for i, (source, part) in enumerate(zip((gate_hbm, up_hbm, down_hbm), parts))
     ]
     stores = [
-        pltpu.make_async_copy(pack_buf.at[part], pack_hbm.at[part], sems.at[1, i])
+        pltpu.make_async_copy(pack_buf.at[part], pack_hbm.at[part], store_sems.at[i])
         for i, part in enumerate(parts)
     ]
-    for load in loads:
-        load.start()
-    halves = cache_wide.shape[0]
-    for h in range(halves):
-        cache_wide[h] = cache_ref[:, h * LANES : (h + 1) * LANES].astype(jnp.float32)
+    for copy in tables + loads:
+        copy.start()
+    tables[0].wait()
     owned = owners_ref[:, 0, :] == lax.axis_index("dp")
-    named = slots_ref[:, 0, :]
     groups, entries = owned.shape
     earlier = lax.broadcasted_iota(jnp.int32, (entries, entries), 0) < lax.broadcasted_iota(
         jnp.int32, (entries, entries), 1
@@ -99,6 +132,8 @@
         jnp.where(earlier, 1.0, 0.0).astype(jnp.bfloat16),
         preferred_element_type=jnp.float32,
     )
+    tables[1].wait()
+    named = slots_ref[:, 0, :]
     held = cache_ref.shape[0] // BLK
     index = lax.broadcasted_iota(jnp.int32, (groups, held), 1)
     picks = []
@@ -106,23 +141,31 @@
         slot = jnp.sum(jnp.where(owned & (rank == r), named, 0), axis=1, keepdims=True)
         picks.append(jnp.where(slot == index, 1.0, 0.0).astype(jnp.bfloat16))
     picks = jnp.concatenate(picks, axis=0)
+    tables[2].wait()
+    halves = cache_wide.shape[0]
+    for h in range(halves):
+        cache_wide[h] = cache_ref[:, h * LANES : (h + 1) * LANES].astype(jnp.float32)
     for load, store in zip(loads, stores):
         load.wait()
         store.start()
-    for b in range(BLK):
-        part = jnp.concatenate(
-            [cache_wide[h, pl.ds(b, held, stride=BLK), :] for h in range(halves)], axis=1
+    outs = []
+    for h in range(halves):
+        for b in range(BLK):
+            part = cache_wide[h, pl.ds(b, held, stride=BLK), :].astype(jnp.bfloat16)
+            chosen = jnp.dot(picks, part, preferred_element_type=jnp.float32)
+            for r in range(OWN_CAP):
+                out_wide[h, pl.ds(r * BLK + b, groups, stride=OWN_CAP * BLK), :] = chosen[
+                    r * groups : (r + 1) * groups
+                ]
+        out_ref[h] = out_wide[h].astype(jnp.bfloat16)
+        outs.append(
+            pltpu.make_async_copy(
+                out_ref.at[h], out_hbm.at[:, pl.ds(h * LANES, LANES)], out_sems.at[h]
+            )
         )
-        chosen = jnp.dot(picks, part.astype(jnp.bfloat16), preferred_element_type=jnp.float32)
-        for r in range(OWN_CAP):
-            for h in range(halves):
-                out_wide[h, pl.ds(r * BLK + b, groups, stride=OWN_CAP * BLK), :] = chosen[
-                    r * groups : (r + 1) * groups, h * LANES : (h + 1) * LANES
-                ]
-    for h in range(halves):
-        out_ref[:, h * LANES : (h + 1) * LANES] = out_wide[h].astype(jnp.bfloat16)
-    for store in stores:
-        store.wait()
+        outs[-1].start()
+    for copy in outs + stores:
+        copy.wait()
 
 
 def norm_kernel(parts_ref, residual_ref, gain_ref, pick_ref, mixed_ref, out_ref):
@@ -238,17 +281,24 @@
     sent_rows = groups * OWN_CAP * BLK
     chosen, packed = pl.pallas_call(
         select_kernel,
-        in_specs=[vmem, vmem, vmem, hbm, hbm, hbm],
-        out_specs=(vmem, hbm),
+        in_specs=[hbm] * 6,
+        out_specs=(hbm, hbm),
         out_shape=(
-            pltpu.VMEM((sent_rows, cache_cols), jnp.bfloat16),
+            pltpu.HBM((sent_rows, cache_cols), jnp.bfloat16),
             pltpu.HBM((3 * unit, width), jnp.bfloat16),
         ),
         scratch_shapes=[
+            pltpu.VMEM((groups, 1, PREF), jnp.int32),
+            pltpu.VMEM((groups, 1, PREF), jnp.int32),
+            pltpu.VMEM((cache_rows, cache_cols), jnp.bfloat16),
             pltpu.VMEM((cache_cols // LANES, cache_rows, LANES), jnp.float32),
             pltpu.VMEM((cache_cols // LANES, sent_rows, LANES), jnp.float32),
+            pltpu.VMEM((cache_cols // LANES, sent_rows, LANES), jnp.bfloat16),
             pltpu.VMEM((3 * unit, width), jnp.bfloat16),
-            pltpu.SemaphoreType.DMA((2, 3)),
+            pltpu.SemaphoreType.DMA((3,)),
+            pltpu.SemaphoreType.DMA((3,)),
+            pltpu.SemaphoreType.DMA((3,)),
+            pltpu.SemaphoreType.DMA((cache_cols // LANES,)),
         ],
         compiler_params=pltpu.CompilerParams(vmem_limit_bytes=12 << 20),
         name="select",
@@ -302,24 +352,54 @@
     ).astype(jnp.bfloat16)
     my_residual = lax.dynamic_slice_in_dim(residual, first, block, 0)
 
+    near = (qkv, out_weight, moe_gain[None, :])
+    near = pl.pallas_call(
+        fetch_kernel,
+        in_specs=[hbm] * len(near),
+        out_specs=(vmem,) * len(near),
+        out_shape=tuple(pltpu.VMEM(x.shape, x.dtype) for x in near),
+        scratch_shapes=[pltpu.SemaphoreType.DMA((len(near),))],
+        compiler_params=pltpu.CompilerParams(vmem_limit_bytes=1 << 20),
+        name="fetch",
+    )(*[in_hbm(x) for x in near])
+    arrived, near, pick_matrix, gate_matrix, my_residual = lax.optimization_barrier(
+        (arrived, near, pick_matrix, gate_matrix, my_residual)
+    )
+    near_qkv, near_weight, near_gain = near
     lines = slots * PIECES
     piece_cols = width // PIECES
-    projected = pl.pallas_call(
+    half = rows // lax.axis_size("section")
+    kept, sent = pl.pallas_call(
         attend_kernel,
         in_specs=[vmem] * 6,
-        out_specs=vmem,
-        out_shape=pltpu.VMEM((rows, width), jnp.bfloat16),
+        out_specs=(vmem, vmem),
+        out_shape=(
+            pltpu.VMEM((half, width), jnp.float32),
+            pltpu.VMEM((half, width), jnp.bfloat16),
+        ),
+        scratch_shapes=[pltpu.VMEM((rows, HEAD_DIM), jnp.bfloat16)],
+        compiler_params=pltpu.CompilerParams(vmem_limit_bytes=16 << 20),
         name="attend",
     )(
-        in_hbm(qkv),
+        in_vmem(near_qkv),
         in_vmem(arrived.reshape(-1, kv_cache.shape[2])),
         in_vmem(key_seg),
         in_hbm(segments[None, :]),
         in_vmem(segments[:, None]),
-        in_hbm(out_weight),
-    )
+        in_vmem(near_weight),
+    )
+    received = lax.ppermute(sent, "section", [(0, 1), (1, 0)])
+    projected = pl.pallas_call(
+        add_kernel,
+        in_specs=[vmem, vmem],
+        out_specs=vmem,
+        out_shape=pltpu.VMEM((half, width), jnp.bfloat16),
+        compiler_params=pltpu.CompilerParams(vmem_limit_bytes=4 << 20),
+        name="add",
+    )(in_vmem(kept), in_vmem(received))
+    chips = lax.axis_size("mp")
     parts = lax.all_to_all(
-        projected.reshape(shards, block, width), SPLIT, split_axis=0, concat_axis=0, tiled=True
+        projected.reshape(chips, block, width), "mp", split_axis=0, concat_axis=0, tiled=True
     )
     mixed, outgoing = pl.pallas_call(
         norm_kernel,
@@ -329,8 +409,9 @@
             pltpu.VMEM((block, width), jnp.float32),
             pltpu.VMEM((lines, piece_cols), jnp.bfloat16),
         ),
+        compiler_params=pltpu.CompilerParams(vmem_limit_bytes=8 << 20),
         name="norm",
-    )(in_vmem(parts), in_vmem(my_residual), in_hbm(moe_gain[None, :]), in_vmem(pick_matrix))
+    )(in_vmem(parts), in_vmem(my_residual), in_vmem(near_gain), in_vmem(pick_matrix))
     incoming = lax.all_to_all(
         outgoing.reshape(groups, CAPQ * PIECES, piece_cols),
         "dp",
@@ -363,6 +444,7 @@
         in_specs=[vmem] * 3,
         out_specs=vmem,
         out_shape=pltpu.VMEM((shards, block, cols), jnp.bfloat16),
+        compiler_params=pltpu.CompilerParams(vmem_limit_bytes=8 << 20),
         name="combine",
     )(in_vmem(returned), in_vmem(gate_matrix), in_vmem(mixed))
     result = lax.all_to_all(finished, SPLIT, split_axis=0, concat_axis=0, tiled=True)

time: 201 us -> 194 us (0.965)
  blocking collectives: 50.7 us -> 97.5 us
  waiting for transfers between devices: 77.7 us -> 34.7 us
  starting transfers between devices: 34.7 us -> 25.5 us
  Pallas kernels: 18.3 us -> 15.5 us
    all_to_all x0 -> x2, blocking collectives: none -> 51.3 us  [the longest x1 38 us: local(): lax.all_to_all(produced.reshape(groups, CAPQ * PIECES, piece_cols), 'dp',...]
    all_to_all x2 -> x0, waiting for transfers between devices: 41.7 us -> none  [the longest x1 29.1 us: local(): lax.all_to_all(produced.reshape(groups, CAPQ * PIECES, piece_cols), 'dp',...]
    all_to_all x2 -> x0, starting transfers between devices: 15.4 us -> none  [the longest x1 8.72 us: local(): lax.all_to_all(projected.reshape(shards, block, width), SPLIT, split_axis...]
    ppermute x0 -> x1, starting transfers between devices: none -> 6.23 us  [local(): received = lax.ppermute(sent, 'section', [(0, 1), (1, 0)])]
    all_to_all x1, blocking collectives: 36.8 us -> 34.3 us  [local(): lax.all_to_all(outgoing.reshape(groups, CAPQ * PIECES, piece_cols), 'dp',...]
    all_to_all x1, waiting for transfers between devices: 36 us -> 33.6 us  [local(): lax.all_to_all(chosen.reshape(groups, OWN_CAP, BLK, cache_cols), 'dp', sp...]
    all_to_all x1, blocking collectives: 13.9 us -> 11.8 us  [local(): lax.all_to_all(finished, SPLIT, split_axis=0, concat_axis=0, tiled=True)]
    pallas_call x2 -> x4, Pallas kernels: 7.49 us -> 6.25 us  [the longest x1 3.19 us: local(): pl.pallas_call(select_kernel, in_specs=[hbm] * 6, out_specs=(hbm, hbm), o...]
  transfers between devices with their start and end apart: 4 -> 3, of which waited for: 3 -> 2; matrix products, arithmetic and copies ran while one was open for 3% -> 3% of each run, Pallas kernels for 2% -> 2%
where the time goes in v3:
time: 194 us; the launch traced here: 193 us
  blocking collectives  97.5 us (50%)
  waiting for transfers between devices  34.7 us (18%)
  starting transfers between devices  25.5 us (13%)
  Pallas kernels  15.5 us (8%)
  between operations  13.6 us (7%)
  local copies, waits for them, and re-layouts  4.06 us (2%)
  other arithmetic  2.31 us (1%)
    all_to_all x1, blocking collectives, local(): lax.all_to_all(produced.reshape(groups, CAPQ * PIECES, piece_cols), 'dp',...  38 us
    all_to_all x1, blocking collectives, local(): lax.all_to_all(outgoing.reshape(groups, CAPQ * PIECES, piece_cols), 'dp',...  34.3 us
    all_to_all x1, waiting for transfers between devices, local(): lax.all_to_all(chosen.reshape(groups, OWN_CAP, BLK, cache_cols), 'dp', sp...  33.6 us
    all_to_all x1, starting transfers between devices, local(): lax.all_to_all(chosen.reshape(groups, OWN_CAP, BLK, cache_cols), 'dp', sp...  19.3 us
    all_to_all x1, blocking collectives, local(): lax.all_to_all(projected.reshape(chips, block, width), 'mp', split_axis=0...  13.3 us
    all_to_all x1, blocking collectives, local(): lax.all_to_all(finished, SPLIT, split_axis=0, concat_axis=0, tiled=True)  11.8 us
    pallas_call x1, Pallas kernels, local(): pl.pallas_call(ffn_kernel, in_specs=[vmem, hbm], out_specs=vmem, out_shap...  8.58 us
    ppermute x1, starting transfers between devices, local(): received = lax.ppermute(sent, 'section', [(0, 1), (1, 0)])  6.23 us
  transfers between devices with their start and end apart: 3, of which 2 were waited for; matrix products, arithmetic and copies ran while one was open for 3% of the time, Pallas kernels for 2%

profile of v3, /device:TPU:1, one launch (start us, length us, event | category | flops | bytes accessed | tf_op | source)
XLA Modules:
  0.0 193.2 jit_solution(14736603381355257146)
XLA Ops:
  6.5 3.2 %select.23 = (bf16[1536,256]{1,0:T(8,128)(2,1)}, bf16[528,2048]{1,0:T(8,128)(2,1)}) custom-call(s32[64,1,64]{2,1,0:T(1,128)} %bitcast.46, s32[64,1,64]{2,1,0:T(1,128)} %slots_hbm.1, bf16[512,256]{1,0:T(8,128)(2,1)} %bitcast.43, bf16[176,2048]{1,0:T(8,128)(2,1)} %bitcast.40, bf16[176,2048]{1,0:T(8,128)(2,1)} %bitcast.41, bf16[176,2048]{1,0:T(8,128)(2,1)} %bitcast.42), custom_call_target="tpu_custom_call" | custom-call | tf_op jit(solution)/shard_map/select/pallas_call | solution.py:282
  9.8 19.3 %all-to-all-start = ((bf16[64,3,8,256]{3,2,1,0:T(8,128)(2,1)}), bf16[64,3,8,256]{3,2,1,0:T(8,128)(2,1)S(1)}, u32[]{:S(2)}, u32[]{:S(2)}) async-start(bf16[64,3,8,256]{3,2,1,0:T(8,128)(2,1)} %bitcast.39), calls=%async_computation | async-start | bytes 1572864 | tf_op jit(solution)/shard_map/all_to_all | solution.py:313
  29.1 0.8 constant_dynamic-slice_fusion.3
  29.8 0.1 copy.27
  29.9 0.1 eq.82
  30.0 0.2 convert_reduce_fusion.1
  30.2 0.1 reduce_sum.48
  30.3 0.1 copy.24
  30.4 0.1 compare_reduce_fusion
  30.5 0.1 copy.25
  30.7 0.8 reduce-window.8
  31.5 0.7 fusion.11
  32.2 0.1 convert_reduce_fusion.2
  32.2 0.2 convert_reduce_fusion
  32.4 0.7 multiply_add_fusion.1
  33.1 0.1 select_reduce_fusion
  33.2 0.8 copy.26.seg_col_ref
  34.0 1.3 fetch.1
  35.3 0.8 constant_dynamic-slice_fusion.2
  36.0 0.1 fusion
  36.2 33.6 %all-to-all-done = bf16[64,3,8,256]{3,2,1,0:T(8,128)(2,1)S(1)} async-done(((bf16[64,3,8,256]{3,2,1,0:T(8,128)(2,1)}), bf16[64,3,8,256]{3,2,1,0:T(8,128)(2,1)S(1)}, u32[]{:S(2)}, u32[]{:S(2)}) %all-to-all-start) | async-done | bytes 786464 | tf_op jit(solution)/shard_map/all_to_all | solution.py:313
  69.8 1.7 attend.1
  71.5 6.2 %collective-permute-start = (bf16[64,2048]{1,0:T(8,128)(2,1)S(1)}, bf16[64,2048]{1,0:T(8,128)(2,1)S(1)}, u32[]{:S(2)}, u32[]{:S(2)}) collective-permute-start(bf16[64,2048]{1,0:T(8,128)(2,1)S(1)} %get-tuple-element.29), channel_id=1, source_target_pairs={{0,256},{256,0},{1,257},{257,1},{2,258},{258,2},{3,259},{259,3},{4... | collective-permute-start | bytes 786440 | tf_op jit(solution)/shard_map/ppermute | solution.py:391
  77.7 1.1 collective-permute-done.b_ref
  78.9 13.3 %all_to_all.25.parts_ref = bf16[4,16,2048]{2,1,0:T(8,128)(2,1)S(1)} all-to-all(bf16[4,16,2048]{2,1,0:T(8,128)(2,1)S(1)} %bitcast.34), channel_id=1, replica_groups=mesh['section'=2,'dp'=64,'mp'=4] {'mp'}, dimensions={0} | all-to-all | bytes 524288 | tf_op jit(solution)/shard_map/all_to_all | solution.py:401
  92.2 0.4 norm.1
  92.7 34.3 %all_to_all.26 = bf16[64,8,512]{2,1,0:T(8,128)(2,1)S(1)} all-to-all(bf16[64,8,512]{2,1,0:T(8,128)(2,1)S(1)} %bitcast.36), channel_id=1, replica_groups=mesh['section'=2,'dp'=64,'mp'=4] {'dp'}, dimensions={0} | all-to-all | bytes 1048576 | tf_op jit(solution)/shard_map/all_to_all | solution.py:415
  126.9 8.6 %ffn.1 = bf16[512,512]{1,0:T(8,128)(2,1)S(1)} custom-call(bf16[512,512]{1,0:T(8,128)(2,1)S(1)} %bitcast.31, bf16[8,3,176,2048]{3,2,1,0:T(8,128)(2,1)} %bitcast.38), custom_call_target="tpu_custom_call" | custom-call | tf_op jit(solution)/shard_map/ffn/pallas_call | solution.py:423
  135.5 38.0 %all_to_all.27 = bf16[64,8,512]{2,1,0:T(8,128)(2,1)S(1)} all-to-all(bf16[64,8,512]{2,1,0:T(8,128)(2,1)S(1)} %bitcast.32), channel_id=1, replica_groups=mesh['section'=2,'dp'=64,'mp'=4] {'dp'}, dimensions={0} | all-to-all | bytes 1048576 | tf_op jit(solution)/shard_map/all_to_all | solution.py:435
  173.6 0.3 combine.1
  173.8 11.8 %all_to_all.28 = bf16[8,16,256]{2,1,0:T(8,128)(2,1)S(1)} all-to-all(bf16[8,16,256]{2,1,0:T(8,128)(2,1)S(1)} %combine.1), channel_id=1, replica_groups=mesh['section'=2,'dp'=64,'mp'=4] {'section','mp'}, dimensions={0} | all-to-all | bytes 131072 | tf_op jit(solution)/shard_map/all_to_all | solution.py:450
  185.7 0.6 copy.29
  (17 shorter events, 0.2 us)
Async XLA Ops:
  6.5 29.6 %copy-start = (bf16[128,2048]{1,0:T(8,128)(2,1)S(1)}, bf16[128,2048]{1,0:T(8,128)(2,1)}, u32[]{:S(2)}) copy-start(bf16[128,2048]{1,0:T(8,128)(2,1)} %param.16) | copy-start | bytes 1572868
  6.5 120.4 %all-gather.2.cloned.1.call-start = ((), (), s32[]{:S(2)}) async-start(), calls=%async_computation.5 | async-start | bytes 19464192 | tf_op jit(solution)/shard_map/all_gather | solution.py:320
  9.8 60.0 %all-to-all-start = ((bf16[64,3,8,256]{3,2,1,0:T(8,128)(2,1)}), bf16[64,3,8,256]{3,2,1,0:T(8,128)(2,1)S(1)}, u32[]{:S(2)}, u32[]{:S(2)}) async-start(bf16[64,3,8,256]{3,2,1,0:T(8,128)(2,1)} %bitcast.39), calls=%async_computation | async-start | bytes 1572864 | tf_op jit(solution)/shard_map/all_to_all | solution.py:313
  71.5 7.4 %collective-permute-start = (bf16[64,2048]{1,0:T(8,128)(2,1)S(1)}, bf16[64,2048]{1,0:T(8,128)(2,1)S(1)}, u32[]{:S(2)}, u32[]{:S(2)}) collective-permute-start(bf16[64,2048]{1,0:T(8,128)(2,1)S(1)} %get-tuple-element.29), channel_id=1, source_target_pairs={{0,256},{256,0},{1,257},{257,1},{2,258},{258,2},{3,259},{259,3},{4... | collective-permute-start | bytes 786440 | tf_op jit(solution)/shard_map/ppermute | solution.py:391
Sparse Core Ops, SparseCore 0:
  9.9 103.3 all-gather.1

commit v4 on v3

--- a/solution.py
+++ b/solution.py
@@ -15,7 +15,8 @@
 OWN_CAP = 3
 CAPQ = 2
 PIECES = 4
-CHUNKS = (2, 2, 2, 1, 1)
+CHUNKS = (4, 4)
+DOWN_PARTS = 2
 SPLIT = ("section", "mp")
 
 
@@ -192,20 +193,29 @@
     return jnp.concatenate([x[i * rows : (i + 1) * rows] for i in range(PIECES)], axis=1)
 
 
-def ffn_kernel(x_ref, weight_hbm, out_ref, weight_ref, sems):
+def ffn_kernel(x_ref, weight_hbm, out_ref, weight_ref, down_ref, hidden_ref, sems, down_sems):
     shards, _, unit, width = weight_ref.shape
     ends = [sum(CHUNKS[: i + 1]) for i in range(len(CHUNKS))]
     spans = [(end - size, size) for end, size in zip(ends, CHUNKS)]
     assert ends[-1] == shards
-    copies = [
+    loads = [
         pltpu.make_async_copy(
-            weight_hbm.at[pl.ds(first, size)], weight_ref.at[pl.ds(first, size)], sems.at[i]
+            weight_hbm.at[pl.ds(first, size), pl.ds(0, 2)],
+            weight_ref.at[pl.ds(first, size)],
+            sems.at[i],
         )
         for i, (first, size) in enumerate(spans)
     ]
-    ahead = 3
-    for copy in copies[:ahead]:
-        copy.start()
+    parts = down_ref.shape[0]
+    cols = width // parts
+    down_loads = [
+        pltpu.make_async_copy(
+            weight_hbm.at[:, 2, :, pl.ds(i * cols, cols)], down_ref.at[i], down_sems.at[i]
+        )
+        for i in range(parts)
+    ]
+    for load in loads + down_loads:
+        load.start()
     total = x_ref.shape[0]
     rows = total // PIECES
     near = lax.broadcasted_iota(jnp.int32, (total, total), 0)
@@ -217,19 +227,26 @@
     x = join_pieces(
         jnp.dot(to_rows, x_ref[...], preferred_element_type=jnp.float32).astype(jnp.bfloat16)
     )
-    result = jnp.zeros((rows, width), jnp.float32)
-    for i, (first, size) in enumerate(spans):
-        copies[i].wait()
-        if i + ahead < len(copies):
-            copies[i + ahead].start()
-        gate, up, down = (
-            weight_ref[first : first + size, j].reshape(size * unit, width) for j in range(3)
+    for load, (first, size) in zip(loads, spans):
+        load.wait()
+        gate, up = (
+            weight_ref[first : first + size, j].reshape(size * unit, width) for j in range(2)
         )
         gate = nt_dot(x, gate)
-        hidden = (gate / (1.0 + jnp.exp(-gate)) * nt_dot(x, up)).astype(jnp.bfloat16)
-        result = result + jnp.dot(hidden, down, preferred_element_type=jnp.float32)
+        hidden_ref[:, first * unit : (first + size) * unit] = (
+            gate / (1.0 + jnp.exp(-gate)) * nt_dot(x, up)
+        ).astype(jnp.bfloat16)
+    result = []
+    for i, load in enumerate(down_loads):
+        load.wait()
+        down = down_ref[i].reshape(shards * unit, cols)
+        result.append(
+            jnp.dot(hidden_ref[...], down, preferred_element_type=jnp.float32).astype(jnp.bfloat16)
+        )
     out_ref[...] = jnp.dot(
-        to_pieces, stack_pieces(result.astype(jnp.bfloat16)), preferred_element_type=jnp.float32
+        to_pieces,
+        stack_pieces(jnp.concatenate(result, axis=1)),
+        preferred_element_type=jnp.float32,
     ).astype(jnp.bfloat16)
 
 
@@ -426,8 +443,11 @@
         out_specs=vmem,
         out_shape=pltpu.VMEM((lines, piece_cols), jnp.bfloat16),
         scratch_shapes=[
-            pltpu.VMEM((shards, 3, unit, width), jnp.bfloat16),
+            pltpu.VMEM((shards, 2, unit, width), jnp.bfloat16),
+            pltpu.VMEM((DOWN_PARTS, shards, unit, width // DOWN_PARTS), jnp.bfloat16),
+            pltpu.VMEM((slots, shards * unit), jnp.bfloat16),
             pltpu.SemaphoreType.DMA((len(CHUNKS),)),
+            pltpu.SemaphoreType.DMA((DOWN_PARTS,)),
         ],
         compiler_params=pltpu.CompilerParams(vmem_limit_bytes=40 << 20),
         name="ffn",

time: 194 us -> 193 us (level)
  no operation moved by 1% of the time
where the time goes in v4:
time: 193 us
  blocking collectives  97.5 us (51%)
  waiting for transfers between devices  34.7 us (18%)
  starting transfers between devices  25.5 us (13%)
  Pallas kernels  14.9 us (8%)
  between operations  13.6 us (7%)
  local copies, waits for them, and re-layouts  4.06 us (2%)
  other arithmetic  2.31 us (1%)
    all_to_all x1, blocking collectives, local(): lax.all_to_all(produced.reshape(groups, CAPQ * PIECES, piece_cols), 'dp',...  38 us
    all_to_all x1, blocking collectives, local(): lax.all_to_all(outgoing.reshape(groups, CAPQ * PIECES, piece_cols), 'dp',...  34.3 us
    all_to_all x1, waiting for transfers between devices, local(): lax.all_to_all(chosen.reshape(groups, OWN_CAP, BLK, cache_cols), 'dp', sp...  33.6 us
    all_to_all x1, starting transfers between devices, local(): lax.all_to_all(chosen.reshape(groups, OWN_CAP, BLK, cache_cols), 'dp', sp...  19.3 us
    all_to_all x1, blocking collectives, local(): lax.all_to_all(projected.reshape(chips, block, width), 'mp', split_axis=0...  13.3 us
    all_to_all x1, blocking collectives, local(): lax.all_to_all(finished, SPLIT, split_axis=0, concat_axis=0, tiled=True)  11.8 us
    pallas_call x1, Pallas kernels, local(): pl.pallas_call(ffn_kernel, in_specs=[vmem, hbm], out_specs=vmem, out_shap...  7.96 us
    ppermute x1, starting transfers between devices, local(): received = lax.ppermute(sent, 'section', [(0, 1), (1, 0)])  6.23 us
  transfers between devices with their start and end apart: 3, of which 2 were waited for; matrix products, arithmetic and copies ran while one was open for 3% of the time, Pallas kernels for 2%

profile of v4, /device:TPU:1, one launch (start us, length us, event | category | flops | bytes accessed | tf_op | source)
XLA Modules:
  0.0 192.6 jit_solution(3577816678672141061)
XLA Ops:
  6.5 3.2 %select.23 = (bf16[1536,256]{1,0:T(8,128)(2,1)}, bf16[528,2048]{1,0:T(8,128)(2,1)}) custom-call(s32[64,1,64]{2,1,0:T(1,128)} %bitcast.46, s32[64,1,64]{2,1,0:T(1,128)} %slots_hbm.1, bf16[512,256]{1,0:T(8,128)(2,1)} %bitcast.43, bf16[176,2048]{1,0:T(8,128)(2,1)} %bitcast.40, bf16[176,2048]{1,0:T(8,128)(2,1)} %bitcast.41, bf16[176,2048]{1,0:T(8,128)(2,1)} %bitcast.42), custom_call_target="tpu_custom_call" | custom-call | tf_op jit(solution)/shard_map/select/pallas_call | solution.py:299
  9.8 19.3 %all-to-all-start = ((bf16[64,3,8,256]{3,2,1,0:T(8,128)(2,1)}), bf16[64,3,8,256]{3,2,1,0:T(8,128)(2,1)S(1)}, u32[]{:S(2)}, u32[]{:S(2)}) async-start(bf16[64,3,8,256]{3,2,1,0:T(8,128)(2,1)} %bitcast.39), calls=%async_computation | async-start | bytes 1572864 | tf_op jit(solution)/shard_map/all_to_all | solution.py:330
  29.1 0.8 constant_dynamic-slice_fusion.3
  29.8 0.1 copy.27
  29.9 0.1 eq.82
  30.0 0.2 convert_reduce_fusion.1
  30.2 0.1 reduce_sum.48
  30.3 0.1 copy.24
  30.4 0.1 compare_reduce_fusion
  30.5 0.1 copy.25
  30.7 0.8 reduce-window.8
  31.5 0.7 fusion.11
  32.2 0.1 convert_reduce_fusion.2
  32.2 0.2 convert_reduce_fusion
  32.4 0.7 multiply_add_fusion.1
  33.1 0.1 select_reduce_fusion
  33.2 0.8 copy.26.seg_col_ref
  34.0 1.3 fetch.1
  35.3 0.8 constant_dynamic-slice_fusion.2
  36.0 0.1 fusion
  36.2 33.6 %all-to-all-done = bf16[64,3,8,256]{3,2,1,0:T(8,128)(2,1)S(1)} async-done(((bf16[64,3,8,256]{3,2,1,0:T(8,128)(2,1)}), bf16[64,3,8,256]{3,2,1,0:T(8,128)(2,1)S(1)}, u32[]{:S(2)}, u32[]{:S(2)}) %all-to-all-start) | async-done | bytes 786464 | tf_op jit(solution)/shard_map/all_to_all | solution.py:330
  69.8 1.7 attend.1
  71.5 6.2 %collective-permute-start = (bf16[64,2048]{1,0:T(8,128)(2,1)S(1)}, bf16[64,2048]{1,0:T(8,128)(2,1)S(1)}, u32[]{:S(2)}, u32[]{:S(2)}) collective-permute-start(bf16[64,2048]{1,0:T(8,128)(2,1)S(1)} %get-tuple-element.29), channel_id=1, source_target_pairs={{0,256},{256,0},{1,257},{257,1},{2,258},{258,2},{3,259},{259,3},{4... | collective-permute-start | bytes 786440 | tf_op jit(solution)/shard_map/ppermute | solution.py:408
  77.7 1.1 collective-permute-done.b_ref
  78.9 13.3 %all_to_all.25.parts_ref = bf16[4,16,2048]{2,1,0:T(8,128)(2,1)S(1)} all-to-all(bf16[4,16,2048]{2,1,0:T(8,128)(2,1)S(1)} %bitcast.34), channel_id=1, replica_groups=mesh['section'=2,'dp'=64,'mp'=4] {'mp'}, dimensions={0} | all-to-all | bytes 524288 | tf_op jit(solution)/shard_map/all_to_all | solution.py:418
  92.2 0.4 norm.1
  92.7 34.3 %all_to_all.26 = bf16[64,8,512]{2,1,0:T(8,128)(2,1)S(1)} all-to-all(bf16[64,8,512]{2,1,0:T(8,128)(2,1)S(1)} %bitcast.36), channel_id=1, replica_groups=mesh['section'=2,'dp'=64,'mp'=4] {'dp'}, dimensions={0} | all-to-all | bytes 1048576 | tf_op jit(solution)/shard_map/all_to_all | solution.py:432
  126.9 8.0 %ffn.1 = bf16[512,512]{1,0:T(8,128)(2,1)S(1)} custom-call(bf16[512,512]{1,0:T(8,128)(2,1)S(1)} %bitcast.31, bf16[8,3,176,2048]{3,2,1,0:T(8,128)(2,1)} %bitcast.38), custom_call_target="tpu_custom_call" | custom-call | tf_op jit(solution)/shard_map/ffn/pallas_call | solution.py:440
  134.9 38.0 %all_to_all.27 = bf16[64,8,512]{2,1,0:T(8,128)(2,1)S(1)} all-to-all(bf16[64,8,512]{2,1,0:T(8,128)(2,1)S(1)} %bitcast.32), channel_id=1, replica_groups=mesh['section'=2,'dp'=64,'mp'=4] {'dp'}, dimensions={0} | all-to-all | bytes 1048576 | tf_op jit(solution)/shard_map/all_to_all | solution.py:455
  172.9 0.3 combine.1
  173.2 11.8 %all_to_all.28 = bf16[8,16,256]{2,1,0:T(8,128)(2,1)S(1)} all-to-all(bf16[8,16,256]{2,1,0:T(8,128)(2,1)S(1)} %combine.1), channel_id=1, replica_groups=mesh['section'=2,'dp'=64,'mp'=4] {'section','mp'}, dimensions={0} | all-to-all | bytes 131072 | tf_op jit(solution)/shard_map/all_to_all | solution.py:470
  185.1 0.6 copy.29
  (17 shorter events, 0.2 us)
Async XLA Ops:
  6.5 29.6 %copy-start = (bf16[128,2048]{1,0:T(8,128)(2,1)S(1)}, bf16[128,2048]{1,0:T(8,128)(2,1)}, u32[]{:S(2)}) copy-start(bf16[128,2048]{1,0:T(8,128)(2,1)} %param.16) | copy-start | bytes 1572868
  6.5 120.4 %all-gather.2.cloned.1.call-start = ((), (), s32[]{:S(2)}) async-start(), calls=%async_computation.5 | async-start | bytes 19464192 | tf_op jit(solution)/shard_map/all_gather | solution.py:337
  9.8 60.0 %all-to-all-start = ((bf16[64,3,8,256]{3,2,1,0:T(8,128)(2,1)}), bf16[64,3,8,256]{3,2,1,0:T(8,128)(2,1)S(1)}, u32[]{:S(2)}, u32[]{:S(2)}) async-start(bf16[64,3,8,256]{3,2,1,0:T(8,128)(2,1)} %bitcast.39), calls=%async_computation | async-start | bytes 1572864 | tf_op jit(solution)/shard_map/all_to_all | solution.py:330
  71.5 7.4 %collective-permute-start = (bf16[64,2048]{1,0:T(8,128)(2,1)S(1)}, bf16[64,2048]{1,0:T(8,128)(2,1)S(1)}, u32[]{:S(2)}, u32[]{:S(2)}) collective-permute-start(bf16[64,2048]{1,0:T(8,128)(2,1)S(1)} %get-tuple-element.29), channel_id=1, source_target_pairs={{0,256},{256,0},{1,257},{257,1},{2,258},{258,2},{3,259},{259,3},{4... | collective-permute-start | bytes 786440 | tf_op jit(solution)/shard_map/ppermute | solution.py:408
Sparse Core Ops, SparseCore 0:
  9.9 103.3 all-gather.1

commit v5 on v4

--- a/solution.py
+++ b/solution.py
@@ -44,12 +44,12 @@
     old = jnp.exp(old - top)
     new = jnp.exp(new - top)
     total = jnp.sum(old, axis=1, keepdims=True) + jnp.sum(new, axis=1, keepdims=True)
-    old = (old / total).astype(jnp.bfloat16)
-    new = (new / total).astype(jnp.bfloat16)
+    old = old.astype(jnp.bfloat16)
+    new = new.astype(jnp.bfloat16)
     attended = jnp.dot(
         old, prefix_ref[:, HEAD_DIM:], preferred_element_type=jnp.float32
     ) + jnp.dot(new, qkv_ref[:, 2 * HEAD_DIM :], preferred_element_type=jnp.float32)
-    rows_ref[...] = attended.astype(jnp.bfloat16)
+    rows_ref[...] = (attended / total).astype(jnp.bfloat16)
     half = keep_ref.shape[0]
     core = lax.axis_index("section")
     for ref, side in ((keep_ref, core), (send_ref, 1 - core)):

time: 193 us -> 193 us (level)
  no operation moved by 1% of the time
where the time goes in v5:
time: 193 us
  blocking collectives  97.9 us (51%)
  waiting for transfers between devices  34.7 us (18%)
  starting transfers between devices  25.5 us (13%)
  Pallas kernels  14.8 us (8%)
  between operations  13.6 us (7%)
  local copies, waits for them, and re-layouts  4.06 us (2%)
  other arithmetic  2.31 us (1%)
    all_to_all x1, blocking collectives, local(): lax.all_to_all(produced.reshape(groups, CAPQ * PIECES, piece_cols), 'dp',...  37.7 us
    all_to_all x1, blocking collectives, local(): lax.all_to_all(outgoing.reshape(groups, CAPQ * PIECES, piece_cols), 'dp',...  35 us
    all_to_all x1, waiting for transfers between devices, local(): lax.all_to_all(chosen.reshape(groups, OWN_CAP, BLK, cache_cols), 'dp', sp...  33.6 us
    all_to_all x1, starting transfers between devices, local(): lax.all_to_all(chosen.reshape(groups, OWN_CAP, BLK, cache_cols), 'dp', sp...  19.3 us
    all_to_all x1, blocking collectives, local(): lax.all_to_all(projected.reshape(chips, block, width), 'mp', split_axis=0...  13.3 us
    all_to_all x1, blocking collectives, local(): lax.all_to_all(finished, SPLIT, split_axis=0, concat_axis=0, tiled=True)  11.8 us
    pallas_call x1, Pallas kernels, local(): pl.pallas_call(ffn_kernel, in_specs=[vmem, hbm], out_specs=vmem, out_shap...  7.96 us
    ppermute x1, starting transfers between devices, local(): received = lax.ppermute(sent, 'section', [(0, 1), (1, 0)])  6.22 us
  transfers between devices with their start and end apart: 3, of which 2 were waited for; matrix products, arithmetic and copies ran while one was open for 3% of the time, Pallas kernels for 2%

profile of v5, /device:TPU:1, one launch (start us, length us, event | category | flops | bytes accessed | tf_op | source)
XLA Modules:
  0.0 192.8 jit_solution(17321101862585776904)
XLA Ops:
  6.5 3.2 %select.23 = (bf16[1536,256]{1,0:T(8,128)(2,1)}, bf16[528,2048]{1,0:T(8,128)(2,1)}) custom-call(s32[64,1,64]{2,1,0:T(1,128)} %bitcast.46, s32[64,1,64]{2,1,0:T(1,128)} %slots_hbm.1, bf16[512,256]{1,0:T(8,128)(2,1)} %bitcast.43, bf16[176,2048]{1,0:T(8,128)(2,1)} %bitcast.40, bf16[176,2048]{1,0:T(8,128)(2,1)} %bitcast.41, bf16[176,2048]{1,0:T(8,128)(2,1)} %bitcast.42), custom_call_target="tpu_custom_call" | custom-call | tf_op jit(solution)/shard_map/select/pallas_call | solution.py:299
  9.8 19.3 %all-to-all-start = ((bf16[64,3,8,256]{3,2,1,0:T(8,128)(2,1)}), bf16[64,3,8,256]{3,2,1,0:T(8,128)(2,1)S(1)}, u32[]{:S(2)}, u32[]{:S(2)}) async-start(bf16[64,3,8,256]{3,2,1,0:T(8,128)(2,1)} %bitcast.39), calls=%async_computation | async-start | bytes 1572864 | tf_op jit(solution)/shard_map/all_to_all | solution.py:330
  29.1 0.8 constant_dynamic-slice_fusion.3
  29.8 0.1 copy.27
  29.9 0.1 eq.82
  30.0 0.2 convert_reduce_fusion.1
  30.2 0.1 reduce_sum.48
  30.3 0.1 copy.24
  30.4 0.1 compare_reduce_fusion
  30.5 0.1 copy.25
  30.7 0.8 reduce-window.8
  31.5 0.7 fusion.11
  32.2 0.1 convert_reduce_fusion.2
  32.2 0.2 convert_reduce_fusion
  32.4 0.7 multiply_add_fusion.1
  33.1 0.1 select_reduce_fusion
  33.2 0.8 copy.26.seg_col_ref
  34.0 1.3 fetch.1
  35.3 0.8 constant_dynamic-slice_fusion.2
  36.0 0.1 fusion
  36.2 33.6 %all-to-all-done = bf16[64,3,8,256]{3,2,1,0:T(8,128)(2,1)S(1)} async-done(((bf16[64,3,8,256]{3,2,1,0:T(8,128)(2,1)}), bf16[64,3,8,256]{3,2,1,0:T(8,128)(2,1)S(1)}, u32[]{:S(2)}, u32[]{:S(2)}) %all-to-all-start) | async-done | bytes 786464 | tf_op jit(solution)/shard_map/all_to_all | solution.py:330
  69.8 1.6 attend.1
  71.4 6.2 %collective-permute-start = (bf16[64,2048]{1,0:T(8,128)(2,1)S(1)}, bf16[64,2048]{1,0:T(8,128)(2,1)S(1)}, u32[]{:S(2)}, u32[]{:S(2)}) collective-permute-start(bf16[64,2048]{1,0:T(8,128)(2,1)S(1)} %get-tuple-element.29), channel_id=1, source_target_pairs={{0,256},{256,0},{1,257},{257,1},{2,258},{258,2},{3,259},{259,3},{4... | collective-permute-start | bytes 786440 | tf_op jit(solution)/shard_map/ppermute | solution.py:408
  77.6 1.1 collective-permute-done.b_ref
  78.8 13.3 %all_to_all.25.parts_ref = bf16[4,16,2048]{2,1,0:T(8,128)(2,1)S(1)} all-to-all(bf16[4,16,2048]{2,1,0:T(8,128)(2,1)S(1)} %bitcast.34), channel_id=1, replica_groups=mesh['section'=2,'dp'=64,'mp'=4] {'mp'}, dimensions={0} | all-to-all | bytes 524288 | tf_op jit(solution)/shard_map/all_to_all | solution.py:418
  92.1 0.4 norm.1
  92.5 35.0 %all_to_all.26 = bf16[64,8,512]{2,1,0:T(8,128)(2,1)S(1)} all-to-all(bf16[64,8,512]{2,1,0:T(8,128)(2,1)S(1)} %bitcast.36), channel_id=1, replica_groups=mesh['section'=2,'dp'=64,'mp'=4] {'dp'}, dimensions={0} | all-to-all | bytes 1048576 | tf_op jit(solution)/shard_map/all_to_all | solution.py:432
  127.6 8.0 %ffn.1 = bf16[512,512]{1,0:T(8,128)(2,1)S(1)} custom-call(bf16[512,512]{1,0:T(8,128)(2,1)S(1)} %bitcast.31, bf16[8,3,176,2048]{3,2,1,0:T(8,128)(2,1)} %bitcast.38), custom_call_target="tpu_custom_call" | custom-call | tf_op jit(solution)/shard_map/ffn/pallas_call | solution.py:440
  135.6 37.7 %all_to_all.27 = bf16[64,8,512]{2,1,0:T(8,128)(2,1)S(1)} all-to-all(bf16[64,8,512]{2,1,0:T(8,128)(2,1)S(1)} %bitcast.32), channel_id=1, replica_groups=mesh['section'=2,'dp'=64,'mp'=4] {'dp'}, dimensions={0} | all-to-all | bytes 1048576 | tf_op jit(solution)/shard_map/all_to_all | solution.py:455
  173.2 0.3 combine.1
  173.5 11.8 %all_to_all.28 = bf16[8,16,256]{2,1,0:T(8,128)(2,1)S(1)} all-to-all(bf16[8,16,256]{2,1,0:T(8,128)(2,1)S(1)} %combine.1), channel_id=1, replica_groups=mesh['section'=2,'dp'=64,'mp'=4] {'section','mp'}, dimensions={0} | all-to-all | bytes 131072 | tf_op jit(solution)/shard_map/all_to_all | solution.py:470
  185.4 0.6 copy.29
  (17 shorter events, 0.2 us)
Async XLA Ops:
  6.5 29.6 %copy-start = (bf16[128,2048]{1,0:T(8,128)(2,1)S(1)}, bf16[128,2048]{1,0:T(8,128)(2,1)}, u32[]{:S(2)}) copy-start(bf16[128,2048]{1,0:T(8,128)(2,1)} %param.16) | copy-start | bytes 1572868
  6.5 121.0 %all-gather.2.cloned.1.call-start = ((), (), s32[]{:S(2)}) async-start(), calls=%async_computation.5 | async-start | bytes 19464192 | tf_op jit(solution)/shard_map/all_gather | solution.py:337
  9.8 60.0 %all-to-all-start = ((bf16[64,3,8,256]{3,2,1,0:T(8,128)(2,1)}), bf16[64,3,8,256]{3,2,1,0:T(8,128)(2,1)S(1)}, u32[]{:S(2)}, u32[]{:S(2)}) async-start(bf16[64,3,8,256]{3,2,1,0:T(8,128)(2,1)} %bitcast.39), calls=%async_computation | async-start | bytes 1572864 | tf_op jit(solution)/shard_map/all_to_all | solution.py:330
  71.4 7.4 %collective-permute-start = (bf16[64,2048]{1,0:T(8,128)(2,1)S(1)}, bf16[64,2048]{1,0:T(8,128)(2,1)S(1)}, u32[]{:S(2)}, u32[]{:S(2)}) collective-permute-start(bf16[64,2048]{1,0:T(8,128)(2,1)S(1)} %get-tuple-element.29), channel_id=1, source_target_pairs={{0,256},{256,0},{1,257},{257,1},{2,258},{258,2},{3,259},{259,3},{4... | collective-permute-start | bytes 786440 | tf_op jit(solution)/shard_map/ppermute | solution.py:408
Sparse Core Ops, SparseCore 0:
  9.9 103.3 all-gather.1
